TPU v7x, 32 devices: a whole 2x2x4 slice. The times are simulated.
32 devices in a mesh: dp: 8 (over z, x), seq: 4 (over y, core).
Axes of the slice: x: 2, y: 2, z: 4, core: 2. Of those that a mesh axis runs over, the one named last changes fastest.
Arguments:
- tokens: bfloat16 [32, 6144], P('dp', 'seq'), may hold values from -6 to 6
- expert_ids: int32 [32, 2], P('dp'), may hold values from 0 to 7, all different within a row; in each aligned block of 4 rows (0 to 3, 4 to 7, ...) at most 2 rows name the same one
- router: bfloat16 [6144, 8], P('seq'), may hold values from -0.21875 to 0.21875
- w_gate: bfloat16 [5, 6144, 16384], P(None, 'seq', 'dp'), may hold values from -0.078125 to 0.078125
- w_up: bfloat16 [5, 6144, 16384], P(None, 'seq', 'dp'), may hold values from -0.078125 to 0.078125
- w_down: bfloat16 [5, 16384, 6144], P(None, 'dp', 'seq'), may hold values from -0.046875 to 0.046875
Outputs:
- mixed: bfloat16 [32, 6144], P('dp', 'seq')
Inputs may be any that keep to these rules, and one draw needn't show every extreme that they name: `expert_ids`: each row names 2 different experts. The 4 tokens of one index of dp name any expert at most 2 times, a bound that some block reaches.
All inputs are finite; a program needn't handle non-finite values.
Results may differ from a plain program's by a relative error of at most 0.0049.
Values may be sent and summed in bfloat16 or wider, within the bound.
No kernel may reach another device: no remote copies, remote signals or barrier semaphores. Data moves between devices by JAX's collectives and lax.ppermute only.
A program may use at most 192 MiB of HBM per device.

v0:
```python
import jax
import jax.numpy as jnp
from jax import lax
from jax.sharding import PartitionSpec as P

MOST = 2


def expert_rows(routes, expert, capacity):
    member = jnp.any(routes == expert, axis=1)
    position = jnp.cumsum(member.astype(jnp.int32)) - 1
    target = jnp.where(member, position, capacity)
    count_all = routes.shape[0]
    row_token = (
        jnp.zeros((capacity,), jnp.int32)
        .at[target]
        .set(jnp.arange(count_all, dtype=jnp.int32), mode="drop")
    )
    live_count = jnp.sum(member.astype(jnp.int32))
    return (row_token, jnp.maximum(position, 0), live_count)


def body(tokens, expert_ids, router, w_gate, w_up, w_down):
    gathered = lax.all_gather(tokens, "dp", axis=0, tiled=True)
    routes = lax.all_gather(expert_ids, "dp", axis=0, tiled=True)
    capacity = MOST * lax.axis_size("dp")
    block_rows = min(128, capacity)
    window_size = w_gate.shape[0]
    buffers = []
    positions = []
    live_blocks = []
    for expert in range(window_size):
        row_token, position, live_count = expert_rows(routes, expert, capacity)
        buffers.append(gathered[row_token])
        positions.append(position)
        live_blocks.append((live_count + block_rows - 1) // block_rows)
    gate_list = []
    up_list = []
    for expert in range(window_size):
        gate_part = jnp.dot(buffers[expert], w_gate[expert], preferred_element_type=jnp.float32)
        up_part = jnp.dot(buffers[expert], w_up[expert], preferred_element_type=jnp.float32)
        gate_list.append(gate_part)
        up_list.append(up_part)
    gate_parts = jnp.stack(gate_list)
    up_parts = jnp.stack(up_list)
    logit_part = jnp.dot(gathered, router, preferred_element_type=jnp.float32)
    gate_sum, up_sum, logits = lax.psum((gate_parts, up_parts, logit_part), "seq")
    hidden = (jax.nn.silu(gate_sum) * up_sum).astype(jnp.bfloat16)
    chosen = jnp.take_along_axis(logits, routes, axis=1)
    share_first = 1.0 / (1.0 + jnp.exp(chosen[:, 1] - chosen[:, 0]))
    share_second = 1.0 / (1.0 + jnp.exp(chosen[:, 0] - chosen[:, 1]))
    partial_value = jnp.zeros((gathered.shape[0], w_down.shape[2]), jnp.float32)
    for expert in range(window_size):
        expert_out = jnp.dot(hidden[expert], w_down[expert], preferred_element_type=jnp.float32)
        weighting = jnp.where(routes[:, 0] == expert, share_first, jnp.float32(0.0))
        weighting = weighting + jnp.where(routes[:, 1] == expert, share_second, jnp.float32(0.0))
        partial_value = partial_value + weighting[:, None] * expert_out[positions[expert]]
    return lax.psum_scatter(partial_value, "dp", scatter_dimension=0, tiled=True).astype(
        jnp.bfloat16
    )


def solution(mesh):
    placed = (
        P("dp", "seq"),
        P("dp", None),
        P("seq", None),
        P(None, "seq", "dp"),
        P(None, "seq", "dp"),
        P(None, "dp", "seq"),
    )
    return jax.shard_map(
        body, mesh=mesh, in_specs=placed, out_specs=P("dp", "seq"), check_vma=False
    )
```

profile of v0, /device:TPU:0, one launch (start us, length us, event | category | flops | bytes accessed | tf_op | source)
XLA Modules:
  0.0 207.5 jit_solution(11027577087069102119)
XLA Ops:
  6.5 22.7 %all-gather = s32[8,4,2]{1,2,0:T(2,128)S(1)} all-gather(s32[1,4,2]{1,2,0:T(2,128)} %bitcast.182), channel_id=1, replica_groups=mesh['dp'=8,'seq'=4] {'dp'}, dimensions={0}, use_global_device_ids=true | all-gather | bytes 288 | tf_op jit(solution)/shard_map/all_gather | solution.py:25
  30.3 0.7 scatter_custom_fusion
  31.3 0.7 scatter_custom_fusion.3
  32.3 0.7 scatter_custom_fusion.2
  33.2 0.7 scatter_custom_fusion.1
  34.2 0.7 scatter_custom_fusion.4
  34.9 30.8 %all-gather.1 = bf16[8,4,1536]{2,1,0:T(4,128)(2,1)S(1)} all-gather(bf16[1,4,1536]{2,1,0:T(4,128)(2,1)} %bitcast.176), channel_id=1, replica_groups=mesh['dp'=8,'seq'=4] {'dp'}, dimensions={0}, use_global_device_ids=true | all-gather | bytes 110592 | tf_op jit(solution)/shard_map/all_gather | solution.py:24
  68.7 3.9 %fusion.48 = f32[5,16,2048]{2,1,0:T(8,128)S(1)} fusion(bf16[16,1536]{1,0:T(8,128)(2,1)S(1)} %gather_fusion, bf16[5,1536,2048]{2,1,0:T(8,128)(2,1)} %param.9), kind=kOutput, calls=%fused_computation.62 | convolution fusion | flops 100663296 | bytes 6471680 | tf_op jit(solution)/shard_map/dot_general | solution.py:40
  72.6 4.4 %fusion.78 = f32[5,16,2048]{2,1,0:T(8,128)S(1)} fusion(bf16[16,1536]{1,0:T(8,128)(2,1)S(1)} %gather_fusion, bf16[5,1536,2048]{2,1,0:T(8,128)(2,1)} %param.10), kind=kOutput, calls=%fused_computation.72 | convolution fusion | flops 100663296 | bytes 6471680 | tf_op jit(solution)/shard_map/dot_general | solution.py:41
  77.0 4.5 %fusion.54 = f32[5,16,2048]{2,1,0:T(8,128)S(1)} fusion(f32[5,16,2048]{2,1,0:T(8,128)S(1)} %fusion.48, bf16[16,1536]{1,0:T(8,128)(2,1)S(1)} %gather_fusion.1, bf16[5,1536,2048]{2,1,0:T(8,128)(2,1)} %param.9), kind=kOutput, calls=%fused_computation.64 | convolution fusion | flops 100663296 | bytes 6471680 | tf_op jit(solution)/shard_map/dot_general | solution.py:40
  81.4 4.5 %fusion.84 = f32[5,16,2048]{2,1,0:T(8,128)S(1)} fusion(f32[5,16,2048]{2,1,0:T(8,128)S(1)} %fusion.78, bf16[16,1536]{1,0:T(8,128)(2,1)S(1)} %gather_fusion.1, bf16[5,1536,2048]{2,1,0:T(8,128)(2,1)} %param.10), kind=kOutput, calls=%fused_computation.74 | convolution fusion | flops 100663296 | bytes 6471680 | tf_op jit(solution)/shard_map/dot_general | solution.py:41
  85.9 3.7 %fusion.60 = f32[5,16,2048]{2,1,0:T(8,128)S(1)} fusion(f32[5,16,2048]{2,1,0:T(8,128)S(1)} %fusion.54, bf16[16,1536]{1,0:T(8,128)(2,1)S(1)} %gather_fusion.2, bf16[5,1536,2048]{2,1,0:T(8,128)(2,1)} %param.9), kind=kOutput, calls=%fused_computation.66 | convolution fusion | flops 100663296 | bytes 6471680 | tf_op jit(solution)/shard_map/dot_general | solution.py:40
  89.6 0.9 fusion.90
  90.6 3.7 %fusion.66 = f32[5,16,2048]{2,1,0:T(8,128)S(1)} fusion(f32[5,16,2048]{2,1,0:T(8,128)S(1)} %fusion.60, bf16[16,1536]{1,0:T(8,128)(2,1)S(1)} %gather_fusion.3, bf16[5,1536,2048]{2,1,0:T(8,128)(2,1)} %param.9), kind=kOutput, calls=%fused_computation.68 | convolution fusion | flops 100663296 | bytes 6471680 | tf_op jit(solution)/shard_map/dot_general | solution.py:40
  94.3 0.9 fusion.96
  95.2 3.7 %fusion.72 = f32[5,16,2048]{2,1,0:T(8,128)S(1)} fusion(f32[5,16,2048]{2,1,0:T(8,128)S(1)} %fusion.66, bf16[16,1536]{1,0:T(8,128)(2,1)S(1)} %gather_fusion.4, bf16[5,1536,2048]{2,1,0:T(8,128)(2,1)} %param.9), kind=kOutput, calls=%fused_computation.70 | convolution fusion | flops 100663296 | bytes 6471680 | tf_op jit(solution)/shard_map/dot_general | solution.py:40
  99.0 0.9 fusion.102
  99.9 0.9 copy-done.2
  101.2 5.7 %psum.21 = f32[32,8]{0,1:T(8,128)S(1)} all-reduce(f32[32,8]{0,1:T(8,128)S(1)} %fusion.120), channel_id=1, replica_groups=mesh['dp'=8,'seq'=4] {'seq'}, use_global_device_ids=true, to_apply=%region_0.0 | all-reduce | flops 256 | bytes 2048 | tf_op jit(solution)/shard_map/psum | solution.py:47
  106.9 0.7 gather_fusion.10
  109.4 28.0 %all-reduce.5.cloned.1.call-done = (f32[5,16,2048]{2,1,0:T(8,128)}, f32[5,16,2048]{2,1,0:T(8,128)}) async-done(((f32[5,16,2048]{2,1,0:T(8,128)}, f32[5,16,2048]{2,1,0:T(8,128)}), (f32[5,16,2048]{2,1,0:T(8,128)}, f32[5,16,2048]{2,1,0:T(8,128)})) %all-reduce.5.cloned.1.call-update) | async-done | bytes 1310736 | tf_op jit(solution)/shard_map/psum | solution.py:47
  137.4 1.5 multiply_convert_fusion
  138.9 3.7 %fusion = f32[16,1536]{1,0:T(8,128)S(1)} fusion(bf16[5,2048,1536]{2,1,0:T(8,128)(2,1)} %param.11, bf16[5,16,2048]{2,1,0:T(8,128)(2,1)S(1)} %multiply_convert_fusion), kind=kOutput, calls=%fused_computation.16 | convolution fusion | flops 100663296 | bytes 6455296 | tf_op jit(solution)/shard_map/dot_general | solution.py:54
  142.6 3.7 %fusion.2 = f32[16,1536]{1,0:T(8,128)S(1)} fusion(bf16[5,2048,1536]{2,1,0:T(8,128)(2,1)} %param.11, bf16[5,16,2048]{2,1,0:T(8,128)(2,1)S(1)} %multiply_convert_fusion), kind=kOutput, calls=%fused_computation.18 | convolution fusion | flops 100663296 | bytes 6455296 | tf_op jit(solution)/shard_map/dot_general | solution.py:54
  146.3 3.7 %fusion.4 = f32[16,1536]{1,0:T(8,128)S(1)} fusion(bf16[5,2048,1536]{2,1,0:T(8,128)(2,1)} %param.11, bf16[5,16,2048]{2,1,0:T(8,128)(2,1)S(1)} %multiply_convert_fusion), kind=kOutput, calls=%fused_computation.20 | convolution fusion | flops 100663296 | bytes 6455296 | tf_op jit(solution)/shard_map/dot_general | solution.py:54
  150.0 3.7 %fusion.6 = f32[16,1536]{1,0:T(8,128)S(1)} fusion(bf16[5,2048,1536]{2,1,0:T(8,128)(2,1)} %param.11, bf16[5,16,2048]{2,1,0:T(8,128)(2,1)S(1)} %multiply_convert_fusion), kind=kOutput, calls=%fused_computation.22 | convolution fusion | flops 100663296 | bytes 6455296 | tf_op jit(solution)/shard_map/dot_general | solution.py:54
  153.7 3.7 %fusion.8 = f32[16,1536]{1,0:T(8,128)S(1)} fusion(bf16[5,2048,1536]{2,1,0:T(8,128)(2,1)} %param.11, bf16[5,16,2048]{2,1,0:T(8,128)(2,1)S(1)} %multiply_convert_fusion), kind=kOutput, calls=%fused_computation.24 | convolution fusion | flops 100663296 | bytes 6455296 | tf_op jit(solution)/shard_map/dot_general | solution.py:54
  157.4 0.6 gather_fusion.9
  158.1 0.6 gather_fusion.8
  158.7 0.6 gather_fusion.7
  159.3 0.6 gather_fusion.5
  160.8 39.3 %all-reduce.6 = bf16[32,1536]{1,0:T(8,128)(2,1)S(1)} all-reduce(f32[32,1536]{1,0:T(8,128)S(1)} %multiply_add_fusion), channel_id=2, replica_groups=mesh['dp'=8,'seq'=4] {'dp'}, use_global_device_ids=true, to_apply=%region_18.19.clone | all-reduce | flops 49152 | bytes 294912
  (77 shorter events, 8.1 us)
Async XLA Ops:
  6.5 94.6 %copy-start = (bf16[1536,8]{0,1:T(8,128)(2,1)S(1)}, bf16[1536,8]{0,1:T(8,128)(2,1)}, u32[]{:S(2)}) copy-start(bf16[1536,8]{0,1:T(8,128)(2,1)} %param.8) | copy-start | bytes 73732
  6.5 130.9 %all-reduce.5.cloned.1.call-start = ((), (), s32[]{:S(2)}) async-start(), calls=%async_computation | async-start | bytes 2621440 | tf_op jit(solution)/shard_map/psum | solution.py:47
  68.7 20.9 %copy-start.1 = (bf16[5,1536,2048]{2,1,0:T(8,128)(2,1)S(1)}, bf16[5,1536,2048]{2,1,0:T(8,128)(2,1)}, u32[]{:S(2)}) copy-start(bf16[5,1536,2048]{2,1,0:T(8,128)(2,1)} %param.10) | copy-start | bytes 94371840
  81.4 26.3 %copy-start.4 = (u32[32]{0:T(128)S(1)}, u32[32]{0:T(128)}, u32[]{:S(2)}) copy-start(u32[32]{0:T(128)} %constant.79) | copy-start | bytes 388
  99.0 0.9 copy-start.3
  99.9 0.9 copy-start.2
Sparse Core Ops, SparseCore 0:
  100.9 36.4 all-reduce.4
where the time goes:
time: 208 us; the launch traced here: 207 us
  blocking collectives  98.3 us (47%)
  matrix products  49.9 us (24%)
  waiting for transfers between devices  28 us (13%)
  between operations  14.4 us (7%)
  local copies, waits for them, and re-layouts  13.9 us (7%)
  other arithmetic  3.05 us (1%)
    unnamed x1, blocking collectives  39.3 us
    all_gather x1, blocking collectives, body(): gathered = lax.all_gather(tokens, 'dp', axis=0, tiled=True)  30.8 us
    psum x1, waiting for transfers between devices, body(): lax.psum((gate_parts, up_parts, logit_part), 'seq')  28 us
    all_gather x1, blocking collectives, body(): routes = lax.all_gather(expert_ids, 'dp', axis=0, tiled=True)  22.7 us
    dot_general x5, matrix products, body(): jnp.dot(buffers[expert], w_gate[expert], preferred_element_type=jnp.float32)  19.5 us
    dot_general x5, matrix products, body(): jnp.dot(hidden[expert], w_down[expert], preferred_element_type=jnp.float32)  18.6 us
    dot_general x5, matrix products, body(): jnp.dot(buffers[expert], w_up[expert], preferred_element_type=jnp.float32)  11.6 us
    psum x1, blocking collectives, body(): lax.psum((gate_parts, up_parts, logit_part), 'seq')  5.66 us
  transfers between devices with their start and end apart: 1, of which 1 were waited for; matrix products, arithmetic and copies ran while one was open for 1% of the time, Pallas kernels for 0%

commit v1 on v0

v1 whole, which is shorter than its diff:
```python
import functools

import jax
import jax.numpy as jnp
from jax import lax
from jax.experimental import pallas as pl
from jax.experimental.pallas import tpu as pltpu
from jax.sharding import PartitionSpec as P


LANES = 128
VMEM = pl.BlockSpec(memory_space=pltpu.VMEM)
HBM = pl.BlockSpec(memory_space=pltpu.HBM)


def swap(value, axis, bit):
    count = lax.axis_size(axis)
    return lax.ppermute(value, axis, [(i, i ^ bit) for i in range(count)])


def half_of(mine):
    core = lax.rem(lax.axis_index("seq"), 2)
    return core if mine else 1 - core


def gate_up_kernel(mine, ahead, x_ref, gate_hbm, up_hbm, out_ref, buffer, sems):
    experts, width, columns = gate_hbm.shape
    half = columns // 2
    start = pl.multiple_of(half_of(mine) * half, half)
    x = x_ref[:, :width]
    first = x_ref[:, width : width + 1].astype(jnp.float32)
    second = x_ref[:, width + 1 : width + 2].astype(jnp.float32)

    def copy(e, kind, slot):
        source = gate_hbm if kind == 0 else up_hbm
        return pltpu.make_async_copy(
            source.at[e, :, pl.ds(start, half)], buffer.at[slot, kind], sems.at[slot, kind]
        )

    for e in range(ahead):
        for kind in range(2):
            copy(e, kind, e).start()
    out_ref[...] = jnp.zeros_like(out_ref)

    @pl.loop(0, experts)
    def _(e):
        slot = lax.rem(e, ahead + 1)
        number = lax.convert_element_type(e, jnp.float32)
        for kind in range(2):
            copy(e, kind, slot).wait()

            @pl.when(e + ahead < experts)
            def _():
                copy(e + ahead, kind, lax.rem(e + ahead, ahead + 1)).start()

            value = jnp.dot(x, buffer[slot, kind], preferred_element_type=jnp.float32)
            for k, named in ((0, first), (1, second)):
                old = out_ref[kind, k].astype(jnp.float32)
                out_ref[kind, k] = jnp.where(named == number, value, old).astype(out_ref.dtype)


def gate_up(mine, x, w_gate, w_up, dtype):
    experts, width, columns = w_gate.shape
    rows, half = x.shape[0], columns // 2
    ahead = min(3, experts)
    return pl.pallas_call(
        functools.partial(gate_up_kernel, mine, ahead),
        out_shape=jax.ShapeDtypeStruct((2, 2, rows, half), dtype),
        in_specs=[VMEM, HBM, HBM],
        out_specs=VMEM,
        scratch_shapes=[
            pltpu.VMEM((ahead + 1, 2, width, half), w_up.dtype),
            pltpu.SemaphoreType.DMA((ahead + 1, 2)),
        ],
        compiler_params=pltpu.CompilerParams(vmem_limit_bytes=40 << 20),
        cost_estimate=pl.CostEstimate(
            flops=2 * rows * experts * width * columns,
            bytes_accessed=2 * experts * width * columns,
            transcendentals=0,
        ),
        name="gate_up_mine" if mine else "gate_up_other",
    )(x, w_gate, w_up)


def hidden_kernel(pair_ref, far_ref, out_ref):
    gate = pair_ref[0] + far_ref[0].astype(jnp.float32)
    up = pair_ref[1] + far_ref[1].astype(jnp.float32)
    out_ref[...] = (gate / (1.0 + jnp.exp(-gate)) * up).astype(out_ref.dtype)


def hidden_of(pair, far):
    return pl.pallas_call(
        hidden_kernel,
        out_shape=jax.ShapeDtypeStruct(pair.shape[1:], far.dtype),
        in_specs=[VMEM, VMEM],
        out_specs=VMEM,
        compiler_params=pltpu.CompilerParams(vmem_limit_bytes=6 << 20),
        cost_estimate=pl.CostEstimate(
            flops=8 * pair.size, bytes_accessed=6 * pair.size, transcendentals=pair.size // 2
        ),
        name="silu_times_up",
    )(pair, far)


def load_kernel(source, gate_ref, out_ref, sems):
    del gate_ref
    copies = [
        pltpu.make_async_copy(source.at[e], out_ref.at[e], sems.at[e])
        for e in range(out_ref.shape[0])
    ]
    for copy in copies:
        copy.start()
    for copy in copies:
        copy.wait()


def load(source, after):
    held = pl.pallas_call(
        load_kernel,
        out_shape=pltpu.VMEM(source.shape, source.dtype),
        in_specs=[HBM, HBM],
        out_specs=VMEM,
        scratch_shapes=[pltpu.SemaphoreType.DMA((source.shape[0],))],
        compiler_params=pltpu.CompilerParams(vmem_limit_bytes=1 << 20),
        cost_estimate=pl.CostEstimate(
            flops=0, bytes_accessed=source.size * source.dtype.itemsize, transcendentals=0
        ),
    )(source, after)
    return held


def down_kernel(mine, last, x_ref, near_ref, far_ref, hidden_ref, down_ref, *rest):
    if last:
        before_ref, keep_ref, send_ref, total_ref = rest
    else:
        (total_ref,) = rest
    experts, columns, width = down_ref.shape
    half = columns // 2
    start = pl.multiple_of(half_of(mine) * half, half)
    rows = x_ref.shape[0]
    first = x_ref[:, width : width + 1].astype(jnp.float32)
    second = x_ref[:, width + 1 : width + 2].astype(jnp.float32)
    logits = near_ref[...] + far_ref[...]
    number = lax.broadcasted_iota(jnp.int32, logits.shape, 1).astype(jnp.float32)
    a = jnp.sum(jnp.where(number == first, logits, 0.0), axis=1, keepdims=True)
    b = jnp.sum(jnp.where(number == second, logits, 0.0), axis=1, keepdims=True)
    share_first = 1.0 / (1.0 + jnp.exp(b - a))
    share_second = 1.0 / (1.0 + jnp.exp(a - b))
    total_ref[...] = before_ref[...] if last else jnp.zeros_like(total_ref)
    h_first = hidden_ref[0].astype(jnp.float32)
    h_second = hidden_ref[1].astype(jnp.float32)

    @pl.loop(0, experts)
    def _(e):
        this = lax.convert_element_type(e, jnp.float32)
        in_first, in_second = first == this, second == this
        h = jnp.where(in_first, h_first, jnp.where(in_second, h_second, 0.0))
        weight = jnp.where(in_first, share_first, jnp.where(in_second, share_second, 0.0))
        out = jnp.dot(
            h.astype(jnp.bfloat16),
            down_ref[e, pl.ds(start, half), :],
            preferred_element_type=jnp.float32,
        )
        total_ref[...] += weight * out

    if last:
        keep_ref[...] = total_ref[: rows // 2]
        send_ref[...] = total_ref[rows // 2 :].astype(send_ref.dtype)


def down(mine, x, near, far, hidden, w_down, before=None):
    experts, columns, width = w_down.shape
    rows = x.shape[0]
    last = before is not None
    operands = [x, near, far, hidden, w_down] + ([before] if last else [])
    if last:
        out_shape = (
            jax.ShapeDtypeStruct((rows // 2, width), jnp.float32),
            jax.ShapeDtypeStruct((rows // 2, width), jnp.float32),
        )
        scratch = [pltpu.VMEM((rows, width), jnp.float32)]
    else:
        out_shape = jax.ShapeDtypeStruct((rows, width), jnp.float32)
        scratch = []
    return pl.pallas_call(
        functools.partial(down_kernel, mine, last),
        out_shape=out_shape,
        in_specs=[VMEM] * len(operands),
        out_specs=(VMEM, VMEM) if last else VMEM,
        scratch_shapes=scratch,
        compiler_params=pltpu.CompilerParams(vmem_limit_bytes=12 << 20),
        cost_estimate=pl.CostEstimate(
            flops=rows * experts * width * columns,
            bytes_accessed=experts * width * columns,
            transcendentals=0,
        ),
        name="down_last" if last else "down_mine",
    )(*operands)


def body(tokens, expert_ids, router, w_gate, w_up, w_down):
    bits = [1 << i for i in range((lax.axis_size("dp") - 1).bit_length())]
    local, width = tokens.shape
    named = jnp.pad(expert_ids.astype(tokens.dtype), ((0, 0), (0, LANES - expert_ids.shape[1])))
    x = lax.optimization_barrier(jnp.concatenate([tokens, named], axis=1))
    for bit in reversed(bits):
        x = jnp.concatenate([x, swap(x, "dp", bit)], axis=0)
        x = lax.optimization_barrier(x)
    logits = jnp.dot(x[:, :width], router, preferred_element_type=jnp.float32)
    logits = logits + swap(logits, "seq", 1)
    other = gate_up(False, x, w_gate, w_up, jnp.float32)
    arrived = swap(other, "seq", 1)
    mine = gate_up(True, x, w_gate, w_up, jnp.float32)
    pair = mine + arrived
    sent = pair.astype(jnp.bfloat16)
    down_fast = load(w_down, sent)
    far_logits = swap(logits, "seq", 2)
    hidden = hidden_of(pair, swap(sent, "seq", 2))
    hidden_other = swap(hidden, "seq", 1)
    part = down(True, x, logits, far_logits, hidden, down_fast)
    total, send = down(False, x, logits, far_logits, hidden_other, down_fast, part)
    for bit in bits:
        total = total + swap(send, "dp", bit)
        if total.shape[0] > local:
            rows = total.shape[0] // 2
            total, send = total[:rows], total[rows:]
    return total.astype(jnp.bfloat16)


def solution(mesh):
    placed = (
        P("dp", "seq"),
        P("dp", None),
        P("seq", None),
        P(None, "seq", "dp"),
        P(None, "seq", "dp"),
        P(None, "dp", "seq"),
    )
    return jax.shard_map(
        body, mesh=mesh, in_specs=placed, out_specs=P("dp", "seq"), check_vma=False
    )
```

time: 208 us -> 102 us (0.49)
  blocking collectives: 98.3 us -> 0 us
  matrix products: 49.9 us -> 0.13 us
  Pallas kernels: 0 us -> 39.4 us
  starting transfers between devices: 0.01 us -> 18.1 us
  between operations: 14.4 us -> 0.14 us
  local copies, waits for them, and re-layouts: 13.9 us -> 20.4 us
  waiting for transfers between devices: 28 us -> 21.7 us
    all_gather x2 -> x0, blocking collectives: 53.4 us -> none  [the longest x1 30.8 us: body(): gathered = lax.all_gather(tokens, 'dp', axis=0, tiled=True)]
    dot_general x16 -> x1, matrix products: 49.9 us -> 0.13 us  [body(): logits = jnp.dot(x[:, :width], router, preferred_element_type=jnp.float32)]
    pallas_call x0 -> x6, Pallas kernels: none -> 39.4 us  [the longest x2 22 us: gate_up(): pl.pallas_call(functools.partial(gate_up_kernel, mine, ahead), out_shape=...]
    unnamed x1 -> x0, blocking collectives: 39.3 us -> none
    psum x1 -> x0, waiting for transfers between devices: 28 us -> none  [body(): lax.psum((gate_parts, up_parts, logit_part), 'seq')]
    ppermute x0 -> x11, waiting for transfers between devices: none -> 21.7 us  [swap(): return lax.ppermute(value, axis, [(i, i ^ bit) for i in range(count)])]
    unnamed x14 -> x6, local copies, waits for them, and re-layouts: 1.67 us -> 20.3 us
    ppermute x0 -> x11, starting transfers between devices: none -> 18.1 us  [swap(): return lax.ppermute(value, axis, [(i, i ^ bit) for i in range(count)])]
  transfers between devices with their start and end apart: 1 -> 11, of which waited for: 1 -> 8; matrix products, arithmetic and copies ran while one was open for 1% -> 0% of each run, Pallas kernels for 0% -> 24%
where the time goes in v1:
time: 102 us
  Pallas kernels  39.4 us (39%)
  waiting for transfers between devices  21.7 us (21%)
  local copies, waits for them, and re-layouts  20.4 us (20%)
  starting transfers between devices  18.1 us (18%)
  other arithmetic  2.15 us (2%)
    pallas_call x2, Pallas kernels, gate_up(): pl.pallas_call(functools.partial(gate_up_kernel, mine, ahead), out_shape=...  22 us
    ppermute x11, waiting for transfers between devices, swap(): return lax.ppermute(value, axis, [(i, i ^ bit) for i in range(count)])  21.7 us
    unnamed x6, local copies, waits for them, and re-layouts  20.3 us
    ppermute x11, starting transfers between devices, swap(): return lax.ppermute(value, axis, [(i, i ^ bit) for i in range(count)])  18.1 us
    pallas_call x1, Pallas kernels, load(): pl.pallas_call(load_kernel, out_shape=pltpu.VMEM(source.shape, source.dty...  10 us
    pallas_call x2, Pallas kernels, down(): pl.pallas_call(functools.partial(down_kernel, mine, last), out_shape=out_...  7.29 us
  transfers between devices with their start and end apart: 11, of which 8 were waited for; matrix products, arithmetic and copies ran while one was open for 0% of the time, Pallas kernels for 24%

profile of v1, /device:TPU:0, one launch (start us, length us, event | category | flops | bytes accessed | tf_op | source)
XLA Modules:
  0.0 102.1 jit_solution(15896536960603798268)
XLA Ops:
  0.0 0.7 convert_element_type.11
  0.7 0.1 copy.10
  0.8 0.7 fusion.4
  1.5 4.1 %collective-permute-start = (bf16[4,1664]{1,0:T(4,128)(2,1)S(1)}, bf16[4,1664]{1,0:T(4,128)(2,1)S(1)}, u32[]{:S(2)}, u32[]{:S(2)}) collective-permute-start(bf16[4,1664]{1,0:T(4,128)(2,1)S(1)} %fusion.4), channel_id=1, source_target_pairs={{0,16},{4,20},{8,24},{12,28},{16,0},{20,4},{24,8},{28,12},{1,17},{... | collective-permute-start | bytes 39944 | tf_op jit(solution)/shard_map/ppermute | solution.py:18
  5.7 1.7 %collective-permute-done = bf16[4,1664]{1,0:T(4,128)(2,1)S(1)} collective-permute-done((bf16[4,1664]{1,0:T(4,128)(2,1)S(1)}, bf16[4,1664]{1,0:T(4,128)(2,1)S(1)}, u32[]{:S(2)}, u32[]{:S(2)}) %collective-permute-start) | collective-permute-done | bytes 13344 | tf_op jit(solution)/shard_map/ppermute | solution.py:18
  7.4 2.0 %collective-permute-start.1 = (bf16[8,1664]{1,0:T(8,128)(2,1)S(1)}, bf16[8,1664]{1,0:T(8,128)(2,1)S(1)}, u32[]{:S(2)}, u32[]{:S(2)}) collective-permute-start(bf16[8,1664]{1,0:T(8,128)(2,1)S(1)} %pad_maximum_fusion.2), channel_id=1, source_target_pairs={{0,8},{4,12},{8,0},{12,4},{16,24},{20,28},{24,16},{28,20},{1,9},{5... | collective-permute-start | bytes 79880 | tf_op jit(solution)/shard_map/ppermute | solution.py:18
  9.3 1.9 %collective-permute-done.1 = bf16[8,1664]{1,0:T(8,128)(2,1)S(1)} collective-permute-done((bf16[8,1664]{1,0:T(8,128)(2,1)S(1)}, bf16[8,1664]{1,0:T(8,128)(2,1)S(1)}, u32[]{:S(2)}, u32[]{:S(2)}) %collective-permute-start.1) | collective-permute-done | bytes 26656 | tf_op jit(solution)/shard_map/ppermute | solution.py:18
  11.3 1.8 %collective-permute-start.2 = (bf16[16,1664]{1,0:T(8,128)(2,1)S(1)}, bf16[16,1664]{1,0:T(8,128)(2,1)S(1)}, u32[]{:S(2)}, u32[]{:S(2)}) collective-permute-start(bf16[16,1664]{1,0:T(8,128)(2,1)S(1)} %pad_maximum_fusion.1), channel_id=1, source_target_pairs={{0,4},{4,0},{8,12},{12,8},{16,20},{20,16},{24,28},{28,24},{1,5},{5... | collective-permute-start | bytes 159752 | tf_op jit(solution)/shard_map/ppermute | solution.py:18
  13.1 2.3 %collective-permute-done.2 = bf16[16,1664]{1,0:T(8,128)(2,1)S(1)} collective-permute-done((bf16[16,1664]{1,0:T(8,128)(2,1)S(1)}, bf16[16,1664]{1,0:T(8,128)(2,1)S(1)}, u32[]{:S(2)}, u32[]{:S(2)}) %collective-permute-start.2) | collective-permute-done | bytes 53280 | tf_op jit(solution)/shard_map/ppermute | solution.py:18
  15.4 11.0 %gate_up_other.1 = f32[2,2,32,1024]{3,2,1,0:T(8,128)S(1)} custom-call(bf16[32,1664]{1,0:T(8,128)(2,1)S(1)} %pad_maximum_fusion.x_ref, bf16[5,1536,2048]{2,1,0:T(8,128)(2,1)} %gate_hbm.3, bf16[5,1536,2048]{2,1,0:T(8,128)(2,1)} %up_hbm.3), custom_call_target="tpu_custom_call" | custom-call | flops 1006632960 | bytes 31457280 | tf_op jit(solution)/shard_map/gate_up_other/pallas_call | solution.py:66
  26.4 0.1 collective-permute-start.5
  26.5 11.0 %gate_up_mine.1 = f32[2,2,32,1024]{3,2,1,0:T(8,128)S(1)} custom-call(bf16[32,1664]{1,0:T(8,128)(2,1)S(1)} %pad_maximum_fusion.x_ref, bf16[5,1536,2048]{2,1,0:T(8,128)(2,1)} %gate_hbm.3, bf16[5,1536,2048]{2,1,0:T(8,128)(2,1)} %up_hbm.3), custom_call_target="tpu_custom_call" | custom-call | flops 1006632960 | bytes 31457280 | tf_op jit(solution)/shard_map/gate_up_mine/pallas_call | solution.py:66
  37.5 0.1 fusion.5
  37.6 1.9 %collective-permute-start.6 = (bf16[2,2,32,1024]{3,2,1,0:T(8,128)(2,1)S(1)}, bf16[2,2,32,1024]{3,2,1,0:T(8,128)(2,1)S(1)}, u32[]{:S(2)}, u32[]{:S(2)}) collective-permute-start(bf16[2,2,32,1024]{3,2,1,0:T(8,128)(2,1)S(1)} %get-tuple-element.9.gate_ref), channel_id=1, source_target_pairs={{0,2},{1,3},{2,0},{3,1},{4,6},{5,7},{6,4},{7,5},{8,10},{9,11},{10,... | collective-permute-start | bytes 786440 | tf_op jit(solution)/shard_map/ppermute | solution.py:18
  39.6 7.0 %collective-permute-done.6.far_ref = bf16[2,2,32,1024]{3,2,1,0:T(8,128)(2,1)S(1)} collective-permute-done((bf16[2,2,32,1024]{3,2,1,0:T(8,128)(2,1)S(1)}, bf16[2,2,32,1024]{3,2,1,0:T(8,128)(2,1)S(1)}, u32[]{:S(2)}, u32[]{:S(2)}) %collective-permute-start.6) | collective-permute-done | bytes 262176 | tf_op jit(solution)/shard_map/ppermute | solution.py:18
  46.5 0.1 silu_times_up.1.hidden_ref
  46.7 0.1 fusion
  46.9 0.5 collective-permute-start.3
  47.4 0.8 collective-permute-done.3
  48.2 1.7 %collective-permute-start.4 = (f32[32,8]{1,0:T(8,128)S(1)}, f32[32,8]{1,0:T(8,128)S(1)}, u32[]{:S(2)}, u32[]{:S(2)}) collective-permute-start(f32[32,8]{1,0:T(8,128)S(1)} %add.17.near_ref), channel_id=1, source_target_pairs={{0,2},{1,3},{2,0},{3,1},{4,6},{5,7},{6,4},{7,5},{8,10},{9,11},{10,... | collective-permute-start | bytes 3080 | tf_op jit(solution)/shard_map/ppermute | solution.py:18
  50.0 10.0 %shard_map.64.down_ref = bf16[5,2048,1536]{2,1,0:T(8,128)(2,1)S(1)} custom-call(bf16[5,2048,1536]{2,1,0:T(8,128)(2,1)} %source.1, bf16[2,2,32,1024]{3,2,1,0:T(8,128)(2,1)S(1)} %get-tuple-element.9.gate_ref), custom_call_target="tpu_custom_call" | custom-call | bytes 31457280 | tf_op jit(solution)/shard_map/pallas_call | solution.py:118
  60.0 3.6 %down_mine.1.rest_0_ = f32[32,1536]{1,0:T(8,128)S(1)} custom-call(bf16[32,1664]{1,0:T(8,128)(2,1)S(1)} %pad_maximum_fusion.x_ref, f32[32,8]{1,0:T(8,128)S(1)} %add.17.near_ref, f32[32,8]{1,0:T(8,128)S(1)} %collective-permute-done.4.far_ref, bf16[2,32,1024]{2,1,0:T(8,128)(2,1)S(1)} %silu_times_up.1.hidden_ref, bf16[5,2048,1536]{2,1,0:T(8,128)(2,1)S(1)} %shard_map.64.down_ref), custom_call_target="tpu_custom_call" | custom-call | flops 503316480 | bytes 15728640 | tf_op jit(solution)/shard_map/down_mine/pallas_call | solution.py:185
  63.7 10.4 %copy-done.1 = bf16[5,2048,1536]{2,1,0:T(8,128)(2,1)} copy-done((bf16[5,2048,1536]{2,1,0:T(8,128)(2,1)}, bf16[5,2048,1536]{2,1,0:T(8,128)(2,1)S(1)}, u32[]{:S(2)}) %copy-start.1) | copy-done | bytes 31457304
  74.0 9.9 %copy-done.2 = bf16[5,2048,1536]{2,1,0:T(8,128)(2,1)S(1)} copy-done((bf16[5,2048,1536]{2,1,0:T(8,128)(2,1)S(1)}, bf16[5,2048,1536]{2,1,0:T(8,128)(2,1)}, u32[]{:S(2)}) %copy-start.2) | copy-done | bytes 31457304
  84.0 3.6 %down_last.1 = (f32[16,1536]{1,0:T(8,128)S(1)}, f32[16,1536]{1,0:T(8,128)S(1)}) custom-call(bf16[32,1664]{1,0:T(8,128)(2,1)S(1)} %pad_maximum_fusion.x_ref, f32[32,8]{1,0:T(8,128)S(1)} %add.17.near_ref, f32[32,8]{1,0:T(8,128)S(1)} %collective-permute-done.4.far_ref, bf16[2,32,1024]{2,1,0:T(8,128)(2,1)S(1)} %collective-permute-done.7.hidden_ref, ...), custom_call_target="tpu_custom_call" | custom-call | flops 503316480 | bytes 15728640 | tf_op jit(solution)/shard_map/down_last/pallas_call | solution.py:185
  87.6 1.6 %collective-permute-start.8 = (f32[16,1536]{1,0:T(8,128)S(1)}, f32[16,1536]{1,0:T(8,128)S(1)}, u32[]{:S(2)}, u32[]{:S(2)}) collective-permute-start(f32[16,1536]{1,0:T(8,128)S(1)} %get-tuple-element.8), channel_id=1, source_target_pairs={{0,4},{4,0},{8,12},{12,8},{16,20},{20,16},{24,28},{28,24},{1,5},{5... | collective-permute-start | bytes 294920 | tf_op jit(solution)/shard_map/ppermute | solution.py:18
  89.2 3.3 %collective-permute-done.8 = f32[16,1536]{1,0:T(8,128)S(1)} collective-permute-done((f32[16,1536]{1,0:T(8,128)S(1)}, f32[16,1536]{1,0:T(8,128)S(1)}, u32[]{:S(2)}, u32[]{:S(2)}) %collective-permute-start.8) | collective-permute-done | bytes 98336 | tf_op jit(solution)/shard_map/ppermute | solution.py:18
  92.5 1.6 %collective-permute-start.9 = (f32[8,1536]{1,0:T(8,128)S(1)}, f32[8,1536]{1,0:T(8,128)S(1)}, u32[]{:S(2)}, u32[]{:S(2)}) collective-permute-start(f32[8,1536]{1,0:T(8,128)S(1)} %slice.22), channel_id=1, source_target_pairs={{0,8},{4,12},{8,0},{12,4},{16,24},{20,28},{24,16},{28,20},{1,9},{5... | collective-permute-start | bytes 147464 | tf_op jit(solution)/shard_map/ppermute | solution.py:18
  94.1 2.5 %collective-permute-done.9 = f32[8,1536]{1,0:T(8,128)S(1)} collective-permute-done((f32[8,1536]{1,0:T(8,128)S(1)}, f32[8,1536]{1,0:T(8,128)S(1)}, u32[]{:S(2)}, u32[]{:S(2)}) %collective-permute-start.9) | collective-permute-done | bytes 49184 | tf_op jit(solution)/shard_map/ppermute | solution.py:18
  96.7 2.6 %collective-permute-start.10 = (f32[4,1536]{1,0:T(4,128)S(1)}, f32[4,1536]{1,0:T(4,128)S(1)}, u32[]{:S(2)}, u32[]{:S(2)}) collective-permute-start(f32[4,1536]{1,0:T(4,128)S(1)} %slice.24), channel_id=1, source_target_pairs={{0,16},{4,20},{8,24},{12,28},{16,0},{20,4},{24,8},{28,12},{1,17},{... | collective-permute-start | bytes 73736 | tf_op jit(solution)/shard_map/ppermute | solution.py:18
  99.3 2.2 %collective-permute-done.10 = f32[4,1536]{1,0:T(4,128)S(1)} collective-permute-done((f32[4,1536]{1,0:T(4,128)S(1)}, f32[4,1536]{1,0:T(4,128)S(1)}, u32[]{:S(2)}, u32[]{:S(2)}) %collective-permute-start.10) | collective-permute-done | bytes 24608 | tf_op jit(solution)/shard_map/ppermute | solution.py:18
  101.5 0.6 fusion.3
  (16 shorter events, 0.2 us)
Async XLA Ops:
  0.0 46.7 %copy-start = (bf16[1536,8]{0,1:T(8,128)(2,1)S(1)}, bf16[1536,8]{0,1:T(8,128)(2,1)}, u32[]{:S(2)}) copy-start(bf16[1536,8]{0,1:T(8,128)(2,1)} %param.8) | copy-start | bytes 73732
  1.5 5.8 %collective-permute-start = (bf16[4,1664]{1,0:T(4,128)(2,1)S(1)}, bf16[4,1664]{1,0:T(4,128)(2,1)S(1)}, u32[]{:S(2)}, u32[]{:S(2)}) collective-permute-start(bf16[4,1664]{1,0:T(4,128)(2,1)S(1)} %fusion.4), channel_id=1, source_target_pairs={{0,16},{4,20},{8,24},{12,28},{16,0},{20,4},{24,8},{28,12},{1,17},{... | collective-permute-start | bytes 39944 | tf_op jit(solution)/shard_map/ppermute | solution.py:18
  7.4 3.9 %collective-permute-start.1 = (bf16[8,1664]{1,0:T(8,128)(2,1)S(1)}, bf16[8,1664]{1,0:T(8,128)(2,1)S(1)}, u32[]{:S(2)}, u32[]{:S(2)}) collective-permute-start(bf16[8,1664]{1,0:T(8,128)(2,1)S(1)} %pad_maximum_fusion.2), channel_id=1, source_target_pairs={{0,8},{4,12},{8,0},{12,4},{16,24},{20,28},{24,16},{28,20},{1,9},{5... | collective-permute-start | bytes 79880 | tf_op jit(solution)/shard_map/ppermute | solution.py:18
  11.3 4.1 %collective-permute-start.2 = (bf16[16,1664]{1,0:T(8,128)(2,1)S(1)}, bf16[16,1664]{1,0:T(8,128)(2,1)S(1)}, u32[]{:S(2)}, u32[]{:S(2)}) collective-permute-start(bf16[16,1664]{1,0:T(8,128)(2,1)S(1)} %pad_maximum_fusion.1), channel_id=1, source_target_pairs={{0,4},{4,0},{8,12},{12,8},{16,20},{20,16},{24,28},{28,24},{1,5},{5... | collective-permute-start | bytes 159752 | tf_op jit(solution)/shard_map/ppermute | solution.py:18
  26.4 11.1 %collective-permute-start.5 = (f32[2,2,32,1024]{3,2,1,0:T(8,128)S(1)}, f32[2,2,32,1024]{3,2,1,0:T(8,128)S(1)}, u32[]{:S(2)}, u32[]{:S(2)}) collective-permute-start(f32[2,2,32,1024]{3,2,1,0:T(8,128)S(1)} %gate_up_other.1), channel_id=1, source_target_pairs={{0,1},{1,0},{2,3},{3,2},{4,5},{5,4},{6,7},{7,6},{8,9},{9,8},{10,11... | collective-permute-start | bytes 1572872 | tf_op jit(solution)/shard_map/ppermute | solution.py:18
  37.6 8.9 %collective-permute-start.6 = (bf16[2,2,32,1024]{3,2,1,0:T(8,128)(2,1)S(1)}, bf16[2,2,32,1024]{3,2,1,0:T(8,128)(2,1)S(1)}, u32[]{:S(2)}, u32[]{:S(2)}) collective-permute-start(bf16[2,2,32,1024]{3,2,1,0:T(8,128)(2,1)S(1)} %get-tuple-element.9.gate_ref), channel_id=1, source_target_pairs={{0,2},{1,3},{2,0},{3,1},{4,6},{5,7},{6,4},{7,5},{8,10},{9,11},{10,... | collective-permute-start | bytes 786440 | tf_op jit(solution)/shard_map/ppermute | solution.py:18
  46.7 27.4 %collective-permute-start.7 = (bf16[2,32,1024]{2,1,0:T(8,128)(2,1)S(1)}, bf16[2,32,1024]{2,1,0:T(8,128)(2,1)S(1)}, u32[]{:S(2)}, u32[]{:S(2)}) collective-permute-start(bf16[2,32,1024]{2,1,0:T(8,128)(2,1)S(1)} %silu_times_up.1.hidden_ref), channel_id=1, source_target_pairs={{0,1},{1,0},{2,3},{3,2},{4,5},{5,4},{6,7},{7,6},{8,9},{9,8},{10,11... | collective-permute-start | bytes 393224 | tf_op jit(solution)/shard_map/ppermute | solution.py:18
  46.9 1.4 %collective-permute-start.3 = (f32[32,8]{1,0:T(8,128)S(1)}, f32[32,8]{1,0:T(8,128)S(1)}, u32[]{:S(2)}, u32[]{:S(2)}) collective-permute-start(f32[32,8]{1,0:T(8,128)S(1)} %fusion), channel_id=1, source_target_pairs={{0,1},{1,0},{2,3},{3,2},{4,5},{5,4},{6,7},{7,6},{8,9},{9,8},{10,11... | collective-permute-start | bytes 3080 | tf_op jit(solution)/shard_map/ppermute | solution.py:18
  48.2 11.8 %collective-permute-start.4 = (f32[32,8]{1,0:T(8,128)S(1)}, f32[32,8]{1,0:T(8,128)S(1)}, u32[]{:S(2)}, u32[]{:S(2)}) collective-permute-start(f32[32,8]{1,0:T(8,128)S(1)} %add.17.near_ref), channel_id=1, source_target_pairs={{0,2},{1,3},{2,0},{3,1},{4,6},{5,7},{6,4},{7,5},{8,10},{9,11},{10,... | collective-permute-start | bytes 3080 | tf_op jit(solution)/shard_map/ppermute | solution.py:18
  63.7 10.4 %copy-start.1 = (bf16[5,2048,1536]{2,1,0:T(8,128)(2,1)}, bf16[5,2048,1536]{2,1,0:T(8,128)(2,1)S(1)}, u32[]{:S(2)}) copy-start(bf16[5,2048,1536]{2,1,0:T(8,128)(2,1)S(1)} %shard_map.64.down_ref) | copy-start | bytes 94371840
  74.0 9.9 %copy-start.2 = (bf16[5,2048,1536]{2,1,0:T(8,128)(2,1)S(1)}, bf16[5,2048,1536]{2,1,0:T(8,128)(2,1)}, u32[]{:S(2)}) copy-start(bf16[5,2048,1536]{2,1,0:T(8,128)(2,1)} %copy-done.1) | copy-start | bytes 94371840
  87.6 4.8 %collective-permute-start.8 = (f32[16,1536]{1,0:T(8,128)S(1)}, f32[16,1536]{1,0:T(8,128)S(1)}, u32[]{:S(2)}, u32[]{:S(2)}) collective-permute-start(f32[16,1536]{1,0:T(8,128)S(1)} %get-tuple-element.8), channel_id=1, source_target_pairs={{0,4},{4,0},{8,12},{12,8},{16,20},{20,16},{24,28},{28,24},{1,5},{5... | collective-permute-start | bytes 294920 | tf_op jit(solution)/shard_map/ppermute | solution.py:18
  92.5 4.2 %collective-permute-start.9 = (f32[8,1536]{1,0:T(8,128)S(1)}, f32[8,1536]{1,0:T(8,128)S(1)}, u32[]{:S(2)}, u32[]{:S(2)}) collective-permute-start(f32[8,1536]{1,0:T(8,128)S(1)} %slice.22), channel_id=1, source_target_pairs={{0,8},{4,12},{8,0},{12,4},{16,24},{20,28},{24,16},{28,20},{1,9},{5... | collective-permute-start | bytes 147464 | tf_op jit(solution)/shard_map/ppermute | solution.py:18
  96.7 4.8 %collective-permute-start.10 = (f32[4,1536]{1,0:T(4,128)S(1)}, f32[4,1536]{1,0:T(4,128)S(1)}, u32[]{:S(2)}, u32[]{:S(2)}) collective-permute-start(f32[4,1536]{1,0:T(4,128)S(1)} %slice.24), channel_id=1, source_target_pairs={{0,16},{4,20},{8,24},{12,28},{16,0},{20,4},{24,8},{28,12},{1,17},{... | collective-permute-start | bytes 73736 | tf_op jit(solution)/shard_map/ppermute | solution.py:18

commit v2 on v1

v2 whole, which is shorter than its diff:
```python
import functools

import jax
import jax.numpy as jnp
from jax import lax
from jax.experimental import pallas as pl
from jax.experimental.pallas import tpu as pltpu
from jax.sharding import PartitionSpec as P


LANES = 128
MIB = 1 << 20
WINDOWS = 3
AHEAD = 2
SLOTS = 8
VMEM = pl.BlockSpec(memory_space=pltpu.VMEM)
SMEM = pl.BlockSpec(memory_space=pltpu.SMEM)
HBM = pl.BlockSpec(memory_space=pltpu.HBM)


def steps_of(count):
    return [1 << i for i in range((count - 1).bit_length())]


def swap(value, axis, bit):
    count = lax.axis_size(axis)
    return lax.ppermute(value, axis, [(i, i ^ bit) for i in range(count)])


def cost(flops, moved):
    return pl.CostEstimate(flops=flops, bytes_accessed=moved, transcendentals=0)


def pack_kernel(token_hbm, id_hbm, out_ref, id_ref, sems):
    rows, width = token_hbm.shape
    token_copy = pltpu.make_async_copy(token_hbm, out_ref.at[:, pl.ds(0, width)], sems.at[0])
    id_copy = pltpu.make_async_copy(id_hbm, id_ref, sems.at[1])
    id_copy.start()
    token_copy.start()
    id_copy.wait()
    row = lax.broadcasted_iota(jnp.int32, (rows, rows), 0)
    lane = lax.broadcasted_iota(jnp.int32, (rows, rows), 1)
    place = lax.broadcasted_iota(jnp.int32, (rows, LANES), 1)
    named = jnp.zeros((rows, LANES), jnp.float32)
    for k in range(id_ref.shape[0]):
        numbers = jnp.broadcast_to(id_ref[k : k + 1, :].astype(jnp.float32), (rows, rows))
        column = jnp.sum(jnp.where(row == lane, numbers, 0.0), axis=1, keepdims=True)
        named = jnp.where(place == k, column, named)
    out_ref[:, width:] = named.astype(out_ref.dtype)
    token_copy.wait()


def pack(tokens, expert_ids):
    rows, width = tokens.shape
    return pl.pallas_call(
        pack_kernel,
        out_shape=jax.ShapeDtypeStruct((rows, width + LANES), tokens.dtype),
        in_specs=[HBM, HBM],
        out_specs=VMEM,
        scratch_shapes=[
            pltpu.VMEM(expert_ids.shape[::-1], expert_ids.dtype),
            pltpu.SemaphoreType.DMA((2,)),
        ],
        compiler_params=pltpu.CompilerParams(vmem_limit_bytes=MIB),
        name="pack",
    )(
        pltpu.with_memory_space_constraint(tokens, pltpu.HBM),
        pltpu.with_memory_space_constraint(expert_ids.T, pltpu.HBM),
    )


def block_copy(gate_hbm, up_hbm, number, kind, ring, sems):
    total, half = 2 * gate_hbm.shape[0], gate_hbm.shape[2] // 2
    core = lax.rem(lax.axis_index("seq"), 2)
    if isinstance(number, int):
        side, place, slot = number // total, number % total, number % ring.shape[0]
    else:
        side, place, slot = number // total, lax.rem(number, total), lax.rem(number, ring.shape[0])
    start = pl.multiple_of((core + 1 - side) % 2 * half, half)
    source = gate_hbm if kind == 0 else up_hbm
    return pltpu.make_async_copy(
        source.at[place // 2, :, pl.ds(start, half)], ring.at[slot], sems.at[slot]
    )


def start_block(gate_hbm, up_hbm, number, ring, sems):
    if isinstance(number, int):
        block_copy(gate_hbm, up_hbm, number, number % 2, ring, sems).start()
        return
    for kind in range(2):

        @pl.when(lax.rem(number, 2) == kind)
        def _():
            block_copy(gate_hbm, up_hbm, number, kind, ring, sems).start()


def load_first_kernel(number, gate_hbm, up_hbm, *refs):
    ring, sems = refs[-2:]
    start_block(gate_hbm, up_hbm, number, ring, sems)
    block_copy(gate_hbm, up_hbm, number, 0, ring, sems).wait()


def load_first(number, w_gate, w_up, ring):
    width, half = w_gate.shape[1], w_gate.shape[2] // 2
    slots = min(SLOTS, 2 * w_gate.shape[0])
    return pl.pallas_call(
        functools.partial(load_first_kernel, number),
        out_shape=pltpu.VMEM((slots, width, half), w_gate.dtype),
        in_specs=[HBM, HBM] + ([] if ring is None else [VMEM]),
        out_specs=VMEM,
        input_output_aliases={} if ring is None else {2: 0},
        scratch_shapes=[pltpu.SemaphoreType.DMA((slots,))],
        compiler_params=pltpu.CompilerParams(vmem_limit_bytes=MIB),
        cost_estimate=cost(0, 2 * width * half),
    )(w_gate, w_up, *([] if ring is None else [ring]))


def gate_up_kernel(begin, held, ahead, x_ref, gate_hbm, up_hbm, *refs):
    out_ref, ring, sems = refs[-3:]
    experts, width, _ = gate_hbm.shape
    total, slots = 2 * experts, ring.shape[0]
    stop = begin + total + ahead
    x = x_ref[:, :width]
    first = x_ref[:, width : width + 1].astype(jnp.float32)
    second = x_ref[:, width + 1 : width + 2].astype(jnp.float32)
    for number in range(begin + held, min(begin + slots - 1, stop)):
        start_block(gate_hbm, up_hbm, number, ring, sems)
    out_ref[...] = jnp.zeros_like(out_ref)

    @pl.loop(begin, begin + total)
    def _(number):
        @pl.when(number >= begin + held)
        def _():
            block_copy(gate_hbm, up_hbm, number, 0, ring, sems).wait()

        later = number + slots - 1

        @pl.when(later < stop)
        def _():
            start_block(gate_hbm, up_hbm, later, ring, sems)

        weights = ring[lax.rem(number, slots)]
        value = jnp.dot(x, weights, preferred_element_type=jnp.float32)
        kind, this = lax.rem(number, 2), ((number - begin) // 2).astype(jnp.float32)
        for k, named in ((0, first), (1, second)):
            out_ref[kind, k] = jnp.where(named == this, value, out_ref[kind, k])

    for number in range(begin + total, stop):
        block_copy(gate_hbm, up_hbm, number, 0, ring, sems).wait()


def gate_up(mine, x, w_gate, w_up, ring, held, ahead):
    experts, width, columns = w_gate.shape
    rows, half = x.shape[0], columns // 2
    slots = ring.shape[0]
    assert held < slots and ahead < slots
    return pl.pallas_call(
        functools.partial(gate_up_kernel, 2 * experts if mine else 0, held, ahead),
        out_shape=(
            jax.ShapeDtypeStruct((2, 2, rows, half), jnp.float32),
            pltpu.VMEM(ring.shape, ring.dtype),
        ),
        in_specs=[VMEM, HBM, HBM, VMEM],
        out_specs=(VMEM, VMEM),
        input_output_aliases={3: 1},
        scratch_shapes=[pltpu.SemaphoreType.DMA((slots,))],
        compiler_params=pltpu.CompilerParams(vmem_limit_bytes=4 * MIB),
        cost_estimate=cost(
            4 * rows * experts * width * half, 2 * (2 * experts - held + ahead) * width * half
        ),
        name="gate_up_mine" if mine else "gate_up_other",
    )(x, w_gate, w_up, ring)


def hidden_kernel(pair_ref, far_ref, out_ref):
    gate = pair_ref[0] + far_ref[0].astype(jnp.float32)
    up = pair_ref[1] + far_ref[1].astype(jnp.float32)
    out_ref[...] = (gate / (1.0 + jnp.exp(-gate)) * up).astype(out_ref.dtype)


def hidden_of(pair, far):
    return pl.pallas_call(
        hidden_kernel,
        out_shape=jax.ShapeDtypeStruct(pair.shape[1:], far.dtype),
        in_specs=[VMEM, VMEM],
        out_specs=VMEM,
        compiler_params=pltpu.CompilerParams(vmem_limit_bytes=6 * MIB),
        cost_estimate=pl.CostEstimate(
            flops=8 * pair.size, bytes_accessed=6 * pair.size, transcendentals=pair.size // 2
        ),
        name="silu_times_up",
    )(pair, far)


def piece_copy(mine, down_hbm, expert, held, sem):
    half = down_hbm.shape[1] // 2
    core = lax.rem(lax.axis_index("seq"), 2)
    start = pl.multiple_of((core if mine else 1 - core) * half, half)
    return pltpu.make_async_copy(down_hbm.at[expert, pl.ds(start, half), :], held.at[expert], sem)


def load_down_kernel(count, down_hbm, mine_ref, other_ref, sems):
    experts = down_hbm.shape[0]
    copies = [piece_copy(True, down_hbm, e, mine_ref, sems.at[e]) for e in range(experts)]
    for e in range(count):
        copies.append(piece_copy(False, down_hbm, e, other_ref, sems.at[experts + e]))
    for copy in copies:
        copy.start()
    for copy in copies:
        copy.wait()


def load_down(w_down, count):
    experts, half, width = w_down.shape[0], w_down.shape[1] // 2, w_down.shape[2]
    side = pltpu.VMEM((experts, half, width), w_down.dtype)
    return pl.pallas_call(
        functools.partial(load_down_kernel, count),
        out_shape=(side, side),
        in_specs=[HBM],
        out_specs=(VMEM, VMEM),
        scratch_shapes=[pltpu.SemaphoreType.DMA((2 * experts,))],
        compiler_params=pltpu.CompilerParams(vmem_limit_bytes=MIB),
        cost_estimate=cost(0, 2 * (experts + count) * half * width),
        name="load_down",
    )(w_down)


def down_kernel(last, begin, count, x_ref, near_ref, far_ref, hidden_ref, down_hbm, *refs):
    if last:
        _, before_ref, keep_ref, send_ref, other_ref, total_ref, sems = refs
        held = other_ref
    else:
        held, _, total_ref, other_ref, sems = refs
    copies = [
        piece_copy(False, down_hbm, begin + i, other_ref, sems.at[i]) for i in range(count)
    ]
    for copy in copies:
        copy.start()
    experts, _, width = down_hbm.shape
    rows = x_ref.shape[0]
    first = x_ref[:, width : width + 1].astype(jnp.float32)
    second = x_ref[:, width + 1 : width + 2].astype(jnp.float32)
    logits = near_ref[...] + far_ref[...]
    number = lax.broadcasted_iota(jnp.int32, logits.shape, 1).astype(jnp.float32)
    a = jnp.sum(jnp.where(number == first, logits, 0.0), axis=1, keepdims=True)
    b = jnp.sum(jnp.where(number == second, logits, 0.0), axis=1, keepdims=True)
    share_first = 1.0 / (1.0 + jnp.exp(b - a))
    share_second = 1.0 / (1.0 + jnp.exp(a - b))
    total_ref[...] = before_ref[...] if last else jnp.zeros_like(total_ref)
    h_first = hidden_ref[0].astype(jnp.float32)
    h_second = hidden_ref[1].astype(jnp.float32)

    @pl.loop(0, experts)
    def _(e):
        if last:
            for i in range(count):
                pl.when(e == begin + i)(copies[i].wait)
        this = e.astype(jnp.float32)
        in_first, in_second = first == this, second == this
        h = jnp.where(in_first, h_first, jnp.where(in_second, h_second, 0.0))
        weight = jnp.where(in_first, share_first, jnp.where(in_second, share_second, 0.0))
        out = jnp.dot(h.astype(jnp.bfloat16), held[e], preferred_element_type=jnp.float32)
        total_ref[...] += weight * out

    if last:
        keep_ref[...] = total_ref[: rows // 2]
        send_ref[...] = total_ref[rows // 2 :].astype(send_ref.dtype)
    else:
        for copy in copies:
            copy.wait()


def down(x, near, far, hidden, w_down, mine, other, begin, count, before=None):
    experts, half, width = w_down.shape[0], w_down.shape[1] // 2, w_down.shape[2]
    rows = x.shape[0]
    last = before is not None
    operands = [x, near, far, hidden, w_down] + ([other, before] if last else [mine, other])
    part = jax.ShapeDtypeStruct((rows // 2 if last else rows, width), jnp.float32)
    sums = [part, jax.ShapeDtypeStruct(part.shape, jnp.bfloat16)] if last else [part]
    sems = pltpu.SemaphoreType.DMA((count,))
    return pl.pallas_call(
        functools.partial(down_kernel, last, begin, count),
        out_shape=tuple(sums + [pltpu.VMEM(other.shape, other.dtype)]),
        in_specs=[VMEM] * 4 + [HBM] + [VMEM] * 2,
        out_specs=tuple([VMEM] * (len(sums) + 1)),
        input_output_aliases={5 if last else 6: len(sums)},
        scratch_shapes=([pltpu.VMEM((rows, width), jnp.float32)] if last else []) + [sems],
        compiler_params=pltpu.CompilerParams(vmem_limit_bytes=4 * MIB),
        cost_estimate=cost(2 * rows * experts * width * half, 2 * count * width * half),
        name="down_last" if last else "down_mine",
    )(*operands)


def body(tokens, expert_ids, router, w_gate, w_up, w_down):
    bits = steps_of(lax.axis_size("dp"))
    local, width = tokens.shape
    experts = w_gate.shape[0]
    w_gate, w_up, w_down = (
        pltpu.with_memory_space_constraint(w, pltpu.HBM) for w in (w_gate, w_up, w_down)
    )
    early = min(WINDOWS, len(bits))
    ring = None
    for i in range(early):
        ring = load_first(i, w_gate, w_up, ring)
    x = pack(tokens, expert_ids)
    for bit in reversed(bits):
        x = jnp.concatenate([x, swap(x, "dp", bit)], axis=0)
        x = lax.optimization_barrier(x)
    logits = jnp.dot(x[:, :width], router, preferred_element_type=jnp.float32)
    logits = logits + swap(logits, "seq", 1)
    other, ring = gate_up(False, x, w_gate, w_up, ring, early, AHEAD)
    arrived = swap(other, "seq", 1)
    mine, _ = gate_up(True, x, w_gate, w_up, ring, AHEAD, 0)
    pair = mine + arrived
    sent = pair.astype(jnp.bfloat16)
    down_mine, down_other = load_down(w_down, 1)
    far_logits = swap(logits, "seq", 2)
    hidden = hidden_of(pair, swap(sent, "seq", 2))
    hidden_other = swap(hidden, "seq", 1)
    middle = 1 + (experts - 1) // 2
    part, down_other = down(
        x, logits, far_logits, hidden, w_down, down_mine, down_other, 1, middle - 1
    )
    total, send, _ = down(
        x, logits, far_logits, hidden_other, w_down, None, down_other, middle, experts - middle, part
    )
    for bit in bits:
        total = total + swap(send, "dp", bit).astype(jnp.float32)
        if total.shape[0] > local:
            rows = total.shape[0] // 2
            total, send = total[:rows], total[rows:]
    return total.astype(jnp.bfloat16)


def solution(mesh):
    placed = (
        P("dp", "seq"),
        P("dp", None),
        P("seq", None),
        P(None, "seq", "dp"),
        P(None, "seq", "dp"),
        P(None, "dp", "seq"),
    )
    return jax.shard_map(
        body, mesh=mesh, in_specs=placed, out_specs=P("dp", "seq"), check_vma=False
    )
```

time: 102 us -> 77.3 us (0.76)
  local copies, waits for them, and re-layouts: 20.4 us -> 0.02 us
  waiting for transfers between devices: 21.7 us -> 19.9 us
  starting transfers between devices: 18.1 us -> 16.6 us
  other arithmetic: 2.15 us -> 0.75 us
    unnamed x6 -> x2, local copies, waits for them, and re-layouts: 20.3 us -> 0.01 us
    ppermute x11, waiting for transfers between devices: 21.7 us -> 19.9 us  [swap(): return lax.ppermute(value, axis, [(i, i ^ bit) for i in range(count)])]
    ppermute x11, starting transfers between devices: 18.1 us -> 16.6 us  [swap(): return lax.ppermute(value, axis, [(i, i ^ bit) for i in range(count)])]
    pallas_call x5 -> x9, Pallas kernels: 39.3 us -> 39.3 us  [the longest x2 18.7 us: gate_up(): pl.pallas_call(functools.partial(gate_up_kernel, 2 * experts if mine else...]
  transfers between devices with their start and end apart: 11 -> 11, of which waited for: 8 -> 7; matrix products, arithmetic and copies ran while one was open for 0% -> 0% of each run, Pallas kernels for 24% -> 33%
where the time goes in v2:
time: 77.3 us; the launch traced here: 77 us
  Pallas kernels  39.4 us (51%)
  waiting for transfers between devices  19.9 us (26%)
  starting transfers between devices  16.6 us (21%)
    ppermute x11, waiting for transfers between devices, swap(): return lax.ppermute(value, axis, [(i, i ^ bit) for i in range(count)])  19.9 us
    pallas_call x2, Pallas kernels, gate_up(): pl.pallas_call(functools.partial(gate_up_kernel, 2 * experts if mine else...  18.7 us
    ppermute x11, starting transfers between devices, swap(): return lax.ppermute(value, axis, [(i, i ^ bit) for i in range(count)])  16.6 us
    pallas_call x2, Pallas kernels, down(): pl.pallas_call(functools.partial(down_kernel, last, begin, count), out_sh...  7.38 us
    pallas_call x1, Pallas kernels, load_down(): pl.pallas_call(functools.partial(load_down_kernel, count), out_shape=(sid...  6.57 us
    pallas_call x3, Pallas kernels, load_first(): pl.pallas_call(functools.partial(load_first_kernel, number), out_shape=pl...  5.91 us
  transfers between devices with their start and end apart: 11, of which 7 were waited for; matrix products, arithmetic and copies ran while one was open for 0% of the time, Pallas kernels for 33%

profile of v2, /device:TPU:0, one launch (start us, length us, event | category | flops | bytes accessed | tf_op | source)
XLA Modules:
  0.0 77.0 jit_solution(6072918554229290959)
XLA Ops:
  0.0 0.8 %pack.1 = bf16[4,1664]{1,0:T(4,128)(2,1)S(1)} custom-call(bf16[4,1536]{1,0:T(4,128)(2,1)} %token_hbm.1, s32[2,4]{1,0:T(2,128)} %bitcast.2), custom_call_target="tpu_custom_call" | custom-call | tf_op jit(solution)/shard_map/pack/pallas_call | solution.py:55
  0.8 4.1 %collective-permute-start = (bf16[4,1664]{1,0:T(4,128)(2,1)S(1)}, bf16[4,1664]{1,0:T(4,128)(2,1)S(1)}, u32[]{:S(2)}, u32[]{:S(2)}) collective-permute-start(bf16[4,1664]{1,0:T(4,128)(2,1)S(1)} %pack.1), channel_id=1, source_target_pairs={{0,16},{4,20},{8,24},{12,28},{16,0},{20,4},{24,8},{28,12},{1,17},{... | collective-permute-start | bytes 39944 | tf_op jit(solution)/shard_map/ppermute | solution.py:27
  4.9 1.7 %collective-permute-done = bf16[4,1664]{1,0:T(4,128)(2,1)S(1)} collective-permute-done((bf16[4,1664]{1,0:T(4,128)(2,1)S(1)}, bf16[4,1664]{1,0:T(4,128)(2,1)S(1)}, u32[]{:S(2)}, u32[]{:S(2)}) %collective-permute-start) | collective-permute-done | bytes 13344 | tf_op jit(solution)/shard_map/ppermute | solution.py:27
  6.6 2.0 %collective-permute-start.1 = (bf16[8,1664]{1,0:T(8,128)(2,1)S(1)}, bf16[8,1664]{1,0:T(8,128)(2,1)S(1)}, u32[]{:S(2)}, u32[]{:S(2)}) collective-permute-start(bf16[8,1664]{1,0:T(8,128)(2,1)S(1)} %pad_maximum_fusion.2), channel_id=1, source_target_pairs={{0,8},{4,12},{8,0},{12,4},{16,24},{20,28},{24,16},{28,20},{1,9},{5... | collective-permute-start | bytes 79880 | tf_op jit(solution)/shard_map/ppermute | solution.py:27
  8.6 1.9 %collective-permute-done.1 = bf16[8,1664]{1,0:T(8,128)(2,1)S(1)} collective-permute-done((bf16[8,1664]{1,0:T(8,128)(2,1)S(1)}, bf16[8,1664]{1,0:T(8,128)(2,1)S(1)}, u32[]{:S(2)}, u32[]{:S(2)}) %collective-permute-start.1) | collective-permute-done | bytes 26656 | tf_op jit(solution)/shard_map/ppermute | solution.py:27
  10.6 1.8 %collective-permute-start.2 = (bf16[16,1664]{1,0:T(8,128)(2,1)S(1)}, bf16[16,1664]{1,0:T(8,128)(2,1)S(1)}, u32[]{:S(2)}, u32[]{:S(2)}) collective-permute-start(bf16[16,1664]{1,0:T(8,128)(2,1)S(1)} %pad_maximum_fusion.1), channel_id=1, source_target_pairs={{0,4},{4,0},{8,12},{12,8},{16,20},{20,16},{24,28},{28,24},{1,5},{5... | collective-permute-start | bytes 159752 | tf_op jit(solution)/shard_map/ppermute | solution.py:27
  12.4 2.0 %shard_map.64.refs_0_ = bf16[8,1536,1024]{2,1,0:T(8,128)(2,1)S(1)} custom-call(bf16[5,1536,2048]{2,1,0:T(8,128)(2,1)} %gate_hbm.9, bf16[5,1536,2048]{2,1,0:T(8,128)(2,1)} %up_hbm.9), custom_call_target="tpu_custom_call" | custom-call | bytes 3145728 | tf_op jit(solution)/shard_map/pallas_call | solution.py:106
  14.4 2.0 %shard_map.65.refs_0_ = bf16[8,1536,1024]{2,1,0:T(8,128)(2,1)S(1)} custom-call(bf16[5,1536,2048]{2,1,0:T(8,128)(2,1)} %gate_hbm.9, bf16[5,1536,2048]{2,1,0:T(8,128)(2,1)} %up_hbm.9, bf16[8,1536,1024]{2,1,0:T(8,128)(2,1)S(1)} %shard_map.64.refs_0_), custom_call_target="tpu_custom_call", output_to_operand_aliasing={{}: (2, {})} | custom-call | bytes 3145728 | tf_op jit(solution)/shard_map/pallas_call | solution.py:106
  16.4 2.0 %shard_map.66.refs_0_ = bf16[8,1536,1024]{2,1,0:T(8,128)(2,1)S(1)} custom-call(bf16[5,1536,2048]{2,1,0:T(8,128)(2,1)} %gate_hbm.9, bf16[5,1536,2048]{2,1,0:T(8,128)(2,1)} %up_hbm.9, bf16[8,1536,1024]{2,1,0:T(8,128)(2,1)S(1)} %shard_map.65.refs_0_), custom_call_target="tpu_custom_call", output_to_operand_aliasing={{}: (2, {})} | custom-call | bytes 3145728 | tf_op jit(solution)/shard_map/pallas_call | solution.py:106
  18.3 0.0 collective-permute-done.2
  18.4 9.5 %gate_up_other.1 = (f32[2,2,32,1024]{3,2,1,0:T(8,128)S(1)}, bf16[8,1536,1024]{2,1,0:T(8,128)(2,1)S(1)}) custom-call(bf16[32,1664]{1,0:T(8,128)(2,1)S(1)} %pad_maximum_fusion.x_ref, bf16[5,1536,2048]{2,1,0:T(8,128)(2,1)} %gate_hbm.9, bf16[5,1536,2048]{2,1,0:T(8,128)(2,1)} %up_hbm.9, ...), custom_call_target="tpu_custom_call", output_to_operand_aliasing={{1}: (3, {})} | custom-call | flops 1006632960 | bytes 28311552 | tf_op jit(solution)/shard_map/gate_up_other/pallas_call | solution.py:157
  27.8 0.1 collective-permute-start.5
  27.9 9.2 %gate_up_mine.1 = (f32[2,2,32,1024]{3,2,1,0:T(8,128)S(1)}, bf16[8,1536,1024]{2,1,0:T(8,128)(2,1)S(1)}) custom-call(bf16[32,1664]{1,0:T(8,128)(2,1)S(1)} %pad_maximum_fusion.x_ref, bf16[5,1536,2048]{2,1,0:T(8,128)(2,1)} %gate_hbm.9, bf16[5,1536,2048]{2,1,0:T(8,128)(2,1)} %up_hbm.9, ...), custom_call_target="tpu_custom_call", output_to_operand_aliasing={{1}: (3, {})} | custom-call | flops 1006632960 | bytes 25165824 | tf_op jit(solution)/shard_map/gate_up_mine/pallas_call | solution.py:157
  37.1 0.1 fusion.3
  37.2 1.6 %collective-permute-start.6 = (bf16[2,2,32,1024]{3,2,1,0:T(8,128)(2,1)S(1)}, bf16[2,2,32,1024]{3,2,1,0:T(8,128)(2,1)S(1)}, u32[]{:S(2)}, u32[]{:S(2)}) collective-permute-start(bf16[2,2,32,1024]{3,2,1,0:T(8,128)(2,1)S(1)} %get-tuple-element.23), channel_id=1, source_target_pairs={{0,2},{1,3},{2,0},{3,1},{4,6},{5,7},{6,4},{7,5},{8,10},{9,11},{10,... | collective-permute-start | bytes 786440 | tf_op jit(solution)/shard_map/ppermute | solution.py:27
  38.8 7.2 %collective-permute-done.6.far_ref = bf16[2,2,32,1024]{3,2,1,0:T(8,128)(2,1)S(1)} collective-permute-done((bf16[2,2,32,1024]{3,2,1,0:T(8,128)(2,1)S(1)}, bf16[2,2,32,1024]{3,2,1,0:T(8,128)(2,1)S(1)}, u32[]{:S(2)}, u32[]{:S(2)}) %collective-permute-start.6) | collective-permute-done | bytes 262176 | tf_op jit(solution)/shard_map/ppermute | solution.py:27
  46.0 0.1 silu_times_up.1.hidden_ref
  46.1 0.1 collective-permute-start.7
  46.2 0.1 fusion
  46.3 0.5 collective-permute-start.3
  46.9 0.8 %collective-permute-done.3 = f32[32,8]{1,0:T(8,128)S(1)} collective-permute-done((f32[32,8]{1,0:T(8,128)S(1)}, f32[32,8]{1,0:T(8,128)S(1)}, u32[]{:S(2)}, u32[]{:S(2)}) %collective-permute-start.3) | collective-permute-done | bytes 1056 | tf_op jit(solution)/shard_map/ppermute | solution.py:27
  47.7 1.5 %collective-permute-start.4 = (f32[32,8]{1,0:T(8,128)S(1)}, f32[32,8]{1,0:T(8,128)S(1)}, u32[]{:S(2)}, u32[]{:S(2)}) collective-permute-start(f32[32,8]{1,0:T(8,128)S(1)} %add.15.near_ref), channel_id=1, source_target_pairs={{0,2},{1,3},{2,0},{3,1},{4,6},{5,7},{6,4},{7,5},{8,10},{9,11},{10,... | collective-permute-start | bytes 3080 | tf_op jit(solution)/shard_map/ppermute | solution.py:27
  49.2 6.6 %load_down.1 = (bf16[5,1024,1536]{2,1,0:T(8,128)(2,1)S(1)}, bf16[5,1024,1536]{2,1,0:T(8,128)(2,1)S(1)}) custom-call(bf16[5,2048,1536]{2,1,0:T(8,128)(2,1)} %down_hbm.5), custom_call_target="tpu_custom_call" | custom-call | bytes 18874368 | tf_op jit(solution)/shard_map/load_down/pallas_call | solution.py:216
  55.8 3.7 %down_mine.1 = (f32[32,1536]{1,0:T(8,128)S(1)}, bf16[5,1024,1536]{2,1,0:T(8,128)(2,1)S(1)}) custom-call(bf16[32,1664]{1,0:T(8,128)(2,1)S(1)} %pad_maximum_fusion.x_ref, f32[32,8]{1,0:T(8,128)S(1)} %add.15.near_ref, f32[32,8]{1,0:T(8,128)S(1)} %collective-permute-done.4.far_ref, ...), custom_call_target="tpu_custom_call", output_to_operand_aliasing={{1}: (6, {})} | custom-call | flops 503316480 | bytes 6291456 | tf_op jit(solution)/shard_map/down_mine/pallas_call | solution.py:281
  59.5 3.7 %down_last.1 = (f32[16,1536]{1,0:T(8,128)S(1)}, bf16[16,1536]{1,0:T(8,128)(2,1)S(1)}, bf16[5,1024,1536]{2,1,0:T(8,128)(2,1)S(1)}) custom-call(bf16[32,1664]{1,0:T(8,128)(2,1)S(1)} %pad_maximum_fusion.x_ref, f32[32,8]{1,0:T(8,128)S(1)} %add.15.near_ref, f32[32,8]{1,0:T(8,128)S(1)} %collective-permute-done.4.far_ref, ...), custom_call_target="tpu_custom_call", output_to_operand_aliasing={{2}: (5, {})} | custom-call | flops 503316480 | bytes 6291456 | tf_op jit(solution)/shard_map/down_last/pallas_call | solution.py:281
  63.2 0.6 collective-permute-start.8
  63.8 3.6 %collective-permute-done.8 = bf16[16,1536]{1,0:T(8,128)(2,1)S(1)} collective-permute-done((bf16[16,1536]{1,0:T(8,128)(2,1)S(1)}, bf16[16,1536]{1,0:T(8,128)(2,1)S(1)}, u32[]{:S(2)}, u32[]{:S(2)}) %collective-permute-start.8) | collective-permute-done | bytes 49184 | tf_op jit(solution)/shard_map/ppermute | solution.py:27
  67.4 1.6 %collective-permute-start.9 = (f32[8,1536]{1,0:T(8,128)S(1)}, f32[8,1536]{1,0:T(8,128)S(1)}, u32[]{:S(2)}, u32[]{:S(2)}) collective-permute-start(f32[8,1536]{1,0:T(8,128)S(1)} %slice.22), channel_id=1, source_target_pairs={{0,8},{4,12},{8,0},{12,4},{16,24},{20,28},{24,16},{28,20},{1,9},{5... | collective-permute-start | bytes 147464 | tf_op jit(solution)/shard_map/ppermute | solution.py:27
  69.0 2.5 %collective-permute-done.9 = f32[8,1536]{1,0:T(8,128)S(1)} collective-permute-done((f32[8,1536]{1,0:T(8,128)S(1)}, f32[8,1536]{1,0:T(8,128)S(1)}, u32[]{:S(2)}, u32[]{:S(2)}) %collective-permute-start.9) | collective-permute-done | bytes 49184 | tf_op jit(solution)/shard_map/ppermute | solution.py:27
  71.6 2.6 %collective-permute-start.10 = (f32[4,1536]{1,0:T(4,128)S(1)}, f32[4,1536]{1,0:T(4,128)S(1)}, u32[]{:S(2)}, u32[]{:S(2)}) collective-permute-start(f32[4,1536]{1,0:T(4,128)S(1)} %slice.24), channel_id=1, source_target_pairs={{0,16},{4,20},{8,24},{12,28},{16,0},{20,4},{24,8},{28,12},{1,17},{... | collective-permute-start | bytes 73736 | tf_op jit(solution)/shard_map/ppermute | solution.py:27
  74.2 2.2 %collective-permute-done.10 = f32[4,1536]{1,0:T(4,128)S(1)} collective-permute-done((f32[4,1536]{1,0:T(4,128)S(1)}, f32[4,1536]{1,0:T(4,128)S(1)}, u32[]{:S(2)}, u32[]{:S(2)}) %collective-permute-start.10) | collective-permute-done | bytes 24608 | tf_op jit(solution)/shard_map/ppermute | solution.py:27
  76.4 0.6 fusion.2
  (13 shorter events, 0.1 us)
Async XLA Ops:
  0.0 46.2 %copy-start = (bf16[1536,8]{0,1:T(8,128)(2,1)S(1)}, bf16[1536,8]{0,1:T(8,128)(2,1)}, u32[]{:S(2)}) copy-start(bf16[1536,8]{0,1:T(8,128)(2,1)} %param.8) | copy-start | bytes 73732
  0.8 5.8 %collective-permute-start = (bf16[4,1664]{1,0:T(4,128)(2,1)S(1)}, bf16[4,1664]{1,0:T(4,128)(2,1)S(1)}, u32[]{:S(2)}, u32[]{:S(2)}) collective-permute-start(bf16[4,1664]{1,0:T(4,128)(2,1)S(1)} %pack.1), channel_id=1, source_target_pairs={{0,16},{4,20},{8,24},{12,28},{16,0},{20,4},{24,8},{28,12},{1,17},{... | collective-permute-start | bytes 39944 | tf_op jit(solution)/shard_map/ppermute | solution.py:27
  6.6 3.9 %collective-permute-start.1 = (bf16[8,1664]{1,0:T(8,128)(2,1)S(1)}, bf16[8,1664]{1,0:T(8,128)(2,1)S(1)}, u32[]{:S(2)}, u32[]{:S(2)}) collective-permute-start(bf16[8,1664]{1,0:T(8,128)(2,1)S(1)} %pad_maximum_fusion.2), channel_id=1, source_target_pairs={{0,8},{4,12},{8,0},{12,4},{16,24},{20,28},{24,16},{28,20},{1,9},{5... | collective-permute-start | bytes 79880 | tf_op jit(solution)/shard_map/ppermute | solution.py:27
  10.6 7.8 %collective-permute-start.2 = (bf16[16,1664]{1,0:T(8,128)(2,1)S(1)}, bf16[16,1664]{1,0:T(8,128)(2,1)S(1)}, u32[]{:S(2)}, u32[]{:S(2)}) collective-permute-start(bf16[16,1664]{1,0:T(8,128)(2,1)S(1)} %pad_maximum_fusion.1), channel_id=1, source_target_pairs={{0,4},{4,0},{8,12},{12,8},{16,20},{20,16},{24,28},{28,24},{1,5},{5... | collective-permute-start | bytes 159752 | tf_op jit(solution)/shard_map/ppermute | solution.py:27
  27.8 9.3 %collective-permute-start.5 = (f32[2,2,32,1024]{3,2,1,0:T(8,128)S(1)}, f32[2,2,32,1024]{3,2,1,0:T(8,128)S(1)}, u32[]{:S(2)}, u32[]{:S(2)}) collective-permute-start(f32[2,2,32,1024]{3,2,1,0:T(8,128)S(1)} %get-tuple-element.16), channel_id=1, source_target_pairs={{0,1},{1,0},{2,3},{3,2},{4,5},{5,4},{6,7},{7,6},{8,9},{9,8},{10,11... | collective-permute-start | bytes 1572872 | tf_op jit(solution)/shard_map/ppermute | solution.py:27
  37.2 8.8 %collective-permute-start.6 = (bf16[2,2,32,1024]{3,2,1,0:T(8,128)(2,1)S(1)}, bf16[2,2,32,1024]{3,2,1,0:T(8,128)(2,1)S(1)}, u32[]{:S(2)}, u32[]{:S(2)}) collective-permute-start(bf16[2,2,32,1024]{3,2,1,0:T(8,128)(2,1)S(1)} %get-tuple-element.23), channel_id=1, source_target_pairs={{0,2},{1,3},{2,0},{3,1},{4,6},{5,7},{6,4},{7,5},{8,10},{9,11},{10,... | collective-permute-start | bytes 786440 | tf_op jit(solution)/shard_map/ppermute | solution.py:27
  46.1 13.4 %collective-permute-start.7 = (bf16[2,32,1024]{2,1,0:T(8,128)(2,1)S(1)}, bf16[2,32,1024]{2,1,0:T(8,128)(2,1)S(1)}, u32[]{:S(2)}, u32[]{:S(2)}) collective-permute-start(bf16[2,32,1024]{2,1,0:T(8,128)(2,1)S(1)} %silu_times_up.1.hidden_ref), channel_id=1, source_target_pairs={{0,1},{1,0},{2,3},{3,2},{4,5},{5,4},{6,7},{7,6},{8,9},{9,8},{10,11... | collective-permute-start | bytes 393224 | tf_op jit(solution)/shard_map/ppermute | solution.py:27
  46.3 1.4 %collective-permute-start.3 = (f32[32,8]{1,0:T(8,128)S(1)}, f32[32,8]{1,0:T(8,128)S(1)}, u32[]{:S(2)}, u32[]{:S(2)}) collective-permute-start(f32[32,8]{1,0:T(8,128)S(1)} %fusion), channel_id=1, source_target_pairs={{0,1},{1,0},{2,3},{3,2},{4,5},{5,4},{6,7},{7,6},{8,9},{9,8},{10,11... | collective-permute-start | bytes 3080 | tf_op jit(solution)/shard_map/ppermute | solution.py:27
  47.7 8.1 %collective-permute-start.4 = (f32[32,8]{1,0:T(8,128)S(1)}, f32[32,8]{1,0:T(8,128)S(1)}, u32[]{:S(2)}, u32[]{:S(2)}) collective-permute-start(f32[32,8]{1,0:T(8,128)S(1)} %add.15.near_ref), channel_id=1, source_target_pairs={{0,2},{1,3},{2,0},{3,1},{4,6},{5,7},{6,4},{7,5},{8,10},{9,11},{10,... | collective-permute-start | bytes 3080 | tf_op jit(solution)/shard_map/ppermute | solution.py:27
  63.2 4.2 %collective-permute-start.8 = (bf16[16,1536]{1,0:T(8,128)(2,1)S(1)}, bf16[16,1536]{1,0:T(8,128)(2,1)S(1)}, u32[]{:S(2)}, u32[]{:S(2)}) collective-permute-start(bf16[16,1536]{1,0:T(8,128)(2,1)S(1)} %get-tuple-element.22), channel_id=1, source_target_pairs={{0,4},{4,0},{8,12},{12,8},{16,20},{20,16},{24,28},{28,24},{1,5},{5... | collective-permute-start | bytes 147464 | tf_op jit(solution)/shard_map/ppermute | solution.py:27
  67.4 4.2 %collective-permute-start.9 = (f32[8,1536]{1,0:T(8,128)S(1)}, f32[8,1536]{1,0:T(8,128)S(1)}, u32[]{:S(2)}, u32[]{:S(2)}) collective-permute-start(f32[8,1536]{1,0:T(8,128)S(1)} %slice.22), channel_id=1, source_target_pairs={{0,8},{4,12},{8,0},{12,4},{16,24},{20,28},{24,16},{28,20},{1,9},{5... | collective-permute-start | bytes 147464 | tf_op jit(solution)/shard_map/ppermute | solution.py:27
  71.6 4.8 %collective-permute-start.10 = (f32[4,1536]{1,0:T(4,128)S(1)}, f32[4,1536]{1,0:T(4,128)S(1)}, u32[]{:S(2)}, u32[]{:S(2)}) collective-permute-start(f32[4,1536]{1,0:T(4,128)S(1)} %slice.24), channel_id=1, source_target_pairs={{0,16},{4,20},{8,24},{12,28},{16,0},{20,4},{24,8},{28,12},{1,17},{... | collective-permute-start | bytes 73736 | tf_op jit(solution)/shard_map/ppermute | solution.py:27

commit v3 on v2

--- a/solution.py
+++ b/solution.py
@@ -115,7 +115,7 @@
     )(w_gate, w_up, *([] if ring is None else [ring]))
 
 
-def gate_up_kernel(begin, held, ahead, x_ref, gate_hbm, up_hbm, *refs):
+def gate_up_kernel(begin, held, ahead, x_ref, gate_hbm, up_hbm, _, *refs):
     out_ref, ring, sems = refs[-3:]
     experts, width, _ = gate_hbm.shape
     total, slots = 2 * experts, ring.shape[0]
@@ -126,6 +126,12 @@
     for number in range(begin + held, min(begin + slots - 1, stop)):
         start_block(gate_hbm, up_hbm, number, ring, sems)
     out_ref[...] = jnp.zeros_like(out_ref)
+    half = ring.shape[2]
+    if len(refs) > 3:
+        router_ref = refs[0]
+        out_ref[0, 0, :, half : half + router_ref.shape[0]] = lax.dot_general(
+            x, router_ref[...], (((1,), (1,)), ((), ())), preferred_element_type=jnp.float32
+        )
 
     @pl.loop(begin, begin + total)
     def _(number):
@@ -143,13 +149,14 @@
         value = jnp.dot(x, weights, preferred_element_type=jnp.float32)
         kind, this = lax.rem(number, 2), ((number - begin) // 2).astype(jnp.float32)
         for k, named in ((0, first), (1, second)):
-            out_ref[kind, k] = jnp.where(named == this, value, out_ref[kind, k])
+            old = out_ref[kind, k, :, :half]
+            out_ref[kind, k, :, :half] = jnp.where(named == this, value, old)
 
     for number in range(begin + total, stop):
         block_copy(gate_hbm, up_hbm, number, 0, ring, sems).wait()
 
 
-def gate_up(mine, x, w_gate, w_up, ring, held, ahead):
+def gate_up(mine, x, w_gate, w_up, ring, held, ahead, router=None):
     experts, width, columns = w_gate.shape
     rows, half = x.shape[0], columns // 2
     slots = ring.shape[0]
@@ -157,10 +164,10 @@
     return pl.pallas_call(
         functools.partial(gate_up_kernel, 2 * experts if mine else 0, held, ahead),
         out_shape=(
-            jax.ShapeDtypeStruct((2, 2, rows, half), jnp.float32),
+            jax.ShapeDtypeStruct((2, 2, rows, half + (0 if mine else LANES)), jnp.float32),
             pltpu.VMEM(ring.shape, ring.dtype),
         ),
-        in_specs=[VMEM, HBM, HBM, VMEM],
+        in_specs=[VMEM, HBM, HBM, VMEM] + ([] if mine else [VMEM]),
         out_specs=(VMEM, VMEM),
         input_output_aliases={3: 1},
         scratch_shapes=[pltpu.SemaphoreType.DMA((slots,))],
@@ -169,7 +176,7 @@
             4 * rows * experts * width * half, 2 * (2 * experts - held + ahead) * width * half
         ),
         name="gate_up_mine" if mine else "gate_up_other",
-    )(x, w_gate, w_up, ring)
+    )(x, w_gate, w_up, ring, *([] if mine else [router.T]))
 
 
 def hidden_kernel(pair_ref, far_ref, out_ref):
@@ -293,7 +300,7 @@
 
 def body(tokens, expert_ids, router, w_gate, w_up, w_down):
     bits = steps_of(lax.axis_size("dp"))
-    local, width = tokens.shape
+    local = tokens.shape[0]
     experts = w_gate.shape[0]
     w_gate, w_up, w_down = (
         pltpu.with_memory_space_constraint(w, pltpu.HBM) for w in (w_gate, w_up, w_down)
@@ -306,12 +313,12 @@
     for bit in reversed(bits):
         x = jnp.concatenate([x, swap(x, "dp", bit)], axis=0)
         x = lax.optimization_barrier(x)
-    logits = jnp.dot(x[:, :width], router, preferred_element_type=jnp.float32)
-    logits = logits + swap(logits, "seq", 1)
-    other, ring = gate_up(False, x, w_gate, w_up, ring, early, AHEAD)
+    other, ring = gate_up(False, x, w_gate, w_up, ring, early, AHEAD, router)
     arrived = swap(other, "seq", 1)
     mine, _ = gate_up(True, x, w_gate, w_up, ring, AHEAD, 0)
-    pair = mine + arrived
+    half, stop = mine.shape[-1], mine.shape[-1] + router.shape[1]
+    pair = mine + arrived[..., :half]
+    logits = other[0, 0, :, half:stop] + arrived[0, 0, :, half:stop]
     sent = pair.astype(jnp.bfloat16)
     down_mine, down_other = load_down(w_down, 1)
     far_logits = swap(logits, "seq", 2)
@@ -328,7 +335,7 @@
         total = total + swap(send, "dp", bit).astype(jnp.float32)
         if total.shape[0] > local:
             rows = total.shape[0] // 2
-            total, send = total[:rows], total[rows:]
+            total, send = total[:rows], total[rows:].astype(jnp.bfloat16)
     return total.astype(jnp.bfloat16)
 
 

time: 77.3 us -> 75.4 us (0.975)
  waiting for transfers between devices: 19.9 us -> 18.7 us
    ppermute x11 -> x10, waiting for transfers between devices: 19.9 us -> 18.7 us  [swap(): return lax.ppermute(value, axis, [(i, i ^ bit) for i in range(count)])]
    ppermute x11 -> x10, starting transfers between devices: 16.6 us -> 16.1 us  [swap(): return lax.ppermute(value, axis, [(i, i ^ bit) for i in range(count)])]
  transfers between devices with their start and end apart: 11 -> 10, of which waited for: 7 -> 6; matrix products, arithmetic and copies ran while one was open for 0% -> 0% of each run, Pallas kernels for 33% -> 34%
where the time goes in v3:
time: 75.4 us; the launch traced here: 75.2 us
  Pallas kernels  39.5 us (52%)
  waiting for transfers between devices  18.7 us (25%)
  starting transfers between devices  16.1 us (21%)
    pallas_call x2, Pallas kernels, gate_up(): pl.pallas_call(functools.partial(gate_up_kernel, 2 * experts if mine else...  18.7 us
    ppermute x10, waiting for transfers between devices, swap(): return lax.ppermute(value, axis, [(i, i ^ bit) for i in range(count)])  18.7 us
    ppermute x10, starting transfers between devices, swap(): return lax.ppermute(value, axis, [(i, i ^ bit) for i in range(count)])  16.1 us
    pallas_call x2, Pallas kernels, down(): pl.pallas_call(functools.partial(down_kernel, last, begin, count), out_sh...  7.39 us
    pallas_call x1, Pallas kernels, load_down(): pl.pallas_call(functools.partial(load_down_kernel, count), out_shape=(sid...  6.57 us
    pallas_call x3, Pallas kernels, load_first(): pl.pallas_call(functools.partial(load_first_kernel, number), out_shape=pl...  5.91 us
  transfers between devices with their start and end apart: 10, of which 6 were waited for; matrix products, arithmetic and copies ran while one was open for 0% of the time, Pallas kernels for 34%

profile of v3, /device:TPU:0, one launch (start us, length us, event | category | flops | bytes accessed | tf_op | source)
XLA Modules:
  0.0 75.2 jit_solution(13543095331149091846)
XLA Ops:
  0.0 0.8 %pack.1 = bf16[4,1664]{1,0:T(4,128)(2,1)S(1)} custom-call(bf16[4,1536]{1,0:T(4,128)(2,1)} %token_hbm.1, s32[2,4]{1,0:T(2,128)} %bitcast.5), custom_call_target="tpu_custom_call" | custom-call | tf_op jit(solution)/shard_map/pack/pallas_call | solution.py:55
  0.8 4.1 %collective-permute-start = (bf16[4,1664]{1,0:T(4,128)(2,1)S(1)}, bf16[4,1664]{1,0:T(4,128)(2,1)S(1)}, u32[]{:S(2)}, u32[]{:S(2)}) collective-permute-start(bf16[4,1664]{1,0:T(4,128)(2,1)S(1)} %pack.1), channel_id=1, source_target_pairs={{0,16},{4,20},{8,24},{12,28},{16,0},{20,4},{24,8},{28,12},{1,17},{... | collective-permute-start | bytes 39944 | tf_op jit(solution)/shard_map/ppermute | solution.py:27
  4.9 1.7 %collective-permute-done = bf16[4,1664]{1,0:T(4,128)(2,1)S(1)} collective-permute-done((bf16[4,1664]{1,0:T(4,128)(2,1)S(1)}, bf16[4,1664]{1,0:T(4,128)(2,1)S(1)}, u32[]{:S(2)}, u32[]{:S(2)}) %collective-permute-start) | collective-permute-done | bytes 13344 | tf_op jit(solution)/shard_map/ppermute | solution.py:27
  6.6 2.0 %collective-permute-start.1 = (bf16[8,1664]{1,0:T(8,128)(2,1)S(1)}, bf16[8,1664]{1,0:T(8,128)(2,1)S(1)}, u32[]{:S(2)}, u32[]{:S(2)}) collective-permute-start(bf16[8,1664]{1,0:T(8,128)(2,1)S(1)} %pad_maximum_fusion.2), channel_id=1, source_target_pairs={{0,8},{4,12},{8,0},{12,4},{16,24},{20,28},{24,16},{28,20},{1,9},{5... | collective-permute-start | bytes 79880 | tf_op jit(solution)/shard_map/ppermute | solution.py:27
  8.6 1.9 %collective-permute-done.1 = bf16[8,1664]{1,0:T(8,128)(2,1)S(1)} collective-permute-done((bf16[8,1664]{1,0:T(8,128)(2,1)S(1)}, bf16[8,1664]{1,0:T(8,128)(2,1)S(1)}, u32[]{:S(2)}, u32[]{:S(2)}) %collective-permute-start.1) | collective-permute-done | bytes 26656 | tf_op jit(solution)/shard_map/ppermute | solution.py:27
  10.5 1.8 %collective-permute-start.2 = (bf16[16,1664]{1,0:T(8,128)(2,1)S(1)}, bf16[16,1664]{1,0:T(8,128)(2,1)S(1)}, u32[]{:S(2)}, u32[]{:S(2)}) collective-permute-start(bf16[16,1664]{1,0:T(8,128)(2,1)S(1)} %pad_maximum_fusion.1), channel_id=1, source_target_pairs={{0,4},{4,0},{8,12},{12,8},{16,20},{20,16},{24,28},{28,24},{1,5},{5... | collective-permute-start | bytes 159752 | tf_op jit(solution)/shard_map/ppermute | solution.py:27
  12.4 2.0 %shard_map.64.refs_0_ = bf16[8,1536,1024]{2,1,0:T(8,128)(2,1)S(1)} custom-call(bf16[5,1536,2048]{2,1,0:T(8,128)(2,1)} %gate_hbm.9, bf16[5,1536,2048]{2,1,0:T(8,128)(2,1)} %up_hbm.9), custom_call_target="tpu_custom_call" | custom-call | bytes 3145728 | tf_op jit(solution)/shard_map/pallas_call | solution.py:106
  14.4 2.0 %shard_map.65.refs_0_ = bf16[8,1536,1024]{2,1,0:T(8,128)(2,1)S(1)} custom-call(bf16[5,1536,2048]{2,1,0:T(8,128)(2,1)} %gate_hbm.9, bf16[5,1536,2048]{2,1,0:T(8,128)(2,1)} %up_hbm.9, bf16[8,1536,1024]{2,1,0:T(8,128)(2,1)S(1)} %shard_map.64.refs_0_), custom_call_target="tpu_custom_call", output_to_operand_aliasing={{}: (2, {})} | custom-call | bytes 3145728 | tf_op jit(solution)/shard_map/pallas_call | solution.py:106
  16.3 0.0 copy-start
  16.4 2.0 %shard_map.66._ = bf16[8,1536,1024]{2,1,0:T(8,128)(2,1)S(1)} custom-call(bf16[5,1536,2048]{2,1,0:T(8,128)(2,1)} %gate_hbm.9, bf16[5,1536,2048]{2,1,0:T(8,128)(2,1)} %up_hbm.9, bf16[8,1536,1024]{2,1,0:T(8,128)(2,1)S(1)} %shard_map.65.refs_0_), custom_call_target="tpu_custom_call", output_to_operand_aliasing={{}: (2, {})} | custom-call | bytes 3145728 | tf_op jit(solution)/shard_map/pallas_call | solution.py:106
  18.3 0.0 collective-permute-done.2
  18.4 9.5 %gate_up_other.1 = (f32[2,2,32,1152]{3,2,1,0:T(8,128)S(1)}, bf16[8,1536,1024]{2,1,0:T(8,128)(2,1)S(1)}) custom-call(bf16[32,1664]{1,0:T(8,128)(2,1)S(1)} %pad_maximum_fusion.x_ref, bf16[5,1536,2048]{2,1,0:T(8,128)(2,1)} %gate_hbm.9, bf16[5,1536,2048]{2,1,0:T(8,128)(2,1)} %up_hbm.9, ...), custom_call_target="tpu_custom_call", output_to_operand_aliasing={{1}: (3, {})} | custom-call | flops 1006632960 | bytes 28311552 | tf_op jit(solution)/shard_map/gate_up_other/pallas_call | solution.py:164
  27.9 0.1 collective-permute-start.3
  27.9 9.2 %gate_up_mine.1 = (f32[2,2,32,1024]{3,2,1,0:T(8,128)S(1)}, bf16[8,1536,1024]{2,1,0:T(8,128)(2,1)S(1)}) custom-call(bf16[32,1664]{1,0:T(8,128)(2,1)S(1)} %pad_maximum_fusion.x_ref, bf16[5,1536,2048]{2,1,0:T(8,128)(2,1)} %gate_hbm.9, bf16[5,1536,2048]{2,1,0:T(8,128)(2,1)} %up_hbm.9, ...), custom_call_target="tpu_custom_call", output_to_operand_aliasing={{1}: (3, {})} | custom-call | flops 1006632960 | bytes 25165824 | tf_op jit(solution)/shard_map/gate_up_mine/pallas_call | solution.py:164
  37.2 0.0 collective-permute-done.3
  37.2 0.1 fusion.2
  37.3 1.6 %collective-permute-start.5 = (bf16[2,2,32,1024]{3,2,1,0:T(8,128)(2,1)S(1)}, bf16[2,2,32,1024]{3,2,1,0:T(8,128)(2,1)S(1)}, u32[]{:S(2)}, u32[]{:S(2)}) collective-permute-start(bf16[2,2,32,1024]{3,2,1,0:T(8,128)(2,1)S(1)} %get-tuple-element.23), channel_id=1, source_target_pairs={{0,2},{1,3},{2,0},{3,1},{4,6},{5,7},{6,4},{7,5},{8,10},{9,11},{10,... | collective-permute-start | bytes 786440 | tf_op jit(solution)/shard_map/ppermute | solution.py:27
  38.8 7.2 %collective-permute-done.5.far_ref = bf16[2,2,32,1024]{3,2,1,0:T(8,128)(2,1)S(1)} collective-permute-done((bf16[2,2,32,1024]{3,2,1,0:T(8,128)(2,1)S(1)}, bf16[2,2,32,1024]{3,2,1,0:T(8,128)(2,1)S(1)}, u32[]{:S(2)}, u32[]{:S(2)}) %collective-permute-start.5) | collective-permute-done | bytes 262176 | tf_op jit(solution)/shard_map/ppermute | solution.py:27
  46.0 0.1 silu_times_up.1.hidden_ref
  46.1 0.1 collective-permute-start.6
  46.2 1.6 %collective-permute-start.4 = (f32[32,8]{1,0:T(8,128)S(1)}, f32[32,8]{1,0:T(8,128)S(1)}, u32[]{:S(2)}, u32[]{:S(2)}) collective-permute-start(f32[32,8]{1,0:T(8,128)S(1)} %fusion.1.near_ref), channel_id=1, source_target_pairs={{0,2},{1,3},{2,0},{3,1},{4,6},{5,7},{6,4},{7,5},{8,10},{9,11},{10,... | collective-permute-start | bytes 3080 | tf_op jit(solution)/shard_map/ppermute | solution.py:27
  47.8 6.6 %load_down.1 = (bf16[5,1024,1536]{2,1,0:T(8,128)(2,1)S(1)}, bf16[5,1024,1536]{2,1,0:T(8,128)(2,1)S(1)}) custom-call(bf16[5,2048,1536]{2,1,0:T(8,128)(2,1)} %down_hbm.5), custom_call_target="tpu_custom_call" | custom-call | bytes 18874368 | tf_op jit(solution)/shard_map/load_down/pallas_call | solution.py:223
  54.4 0.0 collective-permute-done.4.far_ref
  54.4 3.7 %down_mine.1 = (f32[32,1536]{1,0:T(8,128)S(1)}, bf16[5,1024,1536]{2,1,0:T(8,128)(2,1)S(1)}) custom-call(bf16[32,1664]{1,0:T(8,128)(2,1)S(1)} %pad_maximum_fusion.x_ref, f32[32,8]{1,0:T(8,128)S(1)} %fusion.1.near_ref, f32[32,8]{1,0:T(8,128)S(1)} %collective-permute-done.4.far_ref, ...), custom_call_target="tpu_custom_call", output_to_operand_aliasing={{1}: (6, {})} | custom-call | flops 503316480 | bytes 6291456 | tf_op jit(solution)/shard_map/down_mine/pallas_call | solution.py:288
  58.1 3.7 %down_last.1 = (f32[16,1536]{1,0:T(8,128)S(1)}, bf16[16,1536]{1,0:T(8,128)(2,1)S(1)}, bf16[5,1024,1536]{2,1,0:T(8,128)(2,1)S(1)}) custom-call(bf16[32,1664]{1,0:T(8,128)(2,1)S(1)} %pad_maximum_fusion.x_ref, f32[32,8]{1,0:T(8,128)S(1)} %fusion.1.near_ref, f32[32,8]{1,0:T(8,128)S(1)} %collective-permute-done.4.far_ref, ...), custom_call_target="tpu_custom_call", output_to_operand_aliasing={{2}: (5, {})} | custom-call | flops 503316480 | bytes 6291456 | tf_op jit(solution)/shard_map/down_last/pallas_call | solution.py:288
  61.8 0.6 collective-permute-start.7
  62.4 3.6 %collective-permute-done.7 = bf16[16,1536]{1,0:T(8,128)(2,1)S(1)} collective-permute-done((bf16[16,1536]{1,0:T(8,128)(2,1)S(1)}, bf16[16,1536]{1,0:T(8,128)(2,1)S(1)}, u32[]{:S(2)}, u32[]{:S(2)}) %collective-permute-start.7) | collective-permute-done | bytes 49184 | tf_op jit(solution)/shard_map/ppermute | solution.py:27
  66.0 1.6 %collective-permute-start.8 = (bf16[8,1536]{1,0:T(8,128)(2,1)S(1)}, bf16[8,1536]{1,0:T(8,128)(2,1)S(1)}, u32[]{:S(2)}, u32[]{:S(2)}) collective-permute-start(bf16[8,1536]{1,0:T(8,128)(2,1)S(1)} %slice.47), channel_id=1, source_target_pairs={{0,8},{4,12},{8,0},{12,4},{16,24},{20,28},{24,16},{28,20},{1,9},{5... | collective-permute-start | bytes 73736 | tf_op jit(solution)/shard_map/ppermute | solution.py:27
  67.6 2.3 %collective-permute-done.8 = bf16[8,1536]{1,0:T(8,128)(2,1)S(1)} collective-permute-done((bf16[8,1536]{1,0:T(8,128)(2,1)S(1)}, bf16[8,1536]{1,0:T(8,128)(2,1)S(1)}, u32[]{:S(2)}, u32[]{:S(2)}) %collective-permute-start.8) | collective-permute-done | bytes 24608 | tf_op jit(solution)/shard_map/ppermute | solution.py:27
  69.9 2.6 %collective-permute-start.9 = (bf16[4,1536]{1,0:T(4,128)(2,1)S(1)}, bf16[4,1536]{1,0:T(4,128)(2,1)S(1)}, u32[]{:S(2)}, u32[]{:S(2)}) collective-permute-start(bf16[4,1536]{1,0:T(4,128)(2,1)S(1)} %slice.48), channel_id=1, source_target_pairs={{0,16},{4,20},{8,24},{12,28},{16,0},{20,4},{24,8},{28,12},{1,17},{... | collective-permute-start | bytes 36872 | tf_op jit(solution)/shard_map/ppermute | solution.py:27
  72.6 2.0 %collective-permute-done.9 = bf16[4,1536]{1,0:T(4,128)(2,1)S(1)} collective-permute-done((bf16[4,1536]{1,0:T(4,128)(2,1)S(1)}, bf16[4,1536]{1,0:T(4,128)(2,1)S(1)}, u32[]{:S(2)}, u32[]{:S(2)}) %collective-permute-start.9) | collective-permute-done | bytes 12320 | tf_op jit(solution)/shard_map/ppermute | solution.py:27
  74.6 0.6 fusion
  (10 shorter events, 0.1 us)
Async XLA Ops:
  0.8 5.8 %collective-permute-start = (bf16[4,1664]{1,0:T(4,128)(2,1)S(1)}, bf16[4,1664]{1,0:T(4,128)(2,1)S(1)}, u32[]{:S(2)}, u32[]{:S(2)}) collective-permute-start(bf16[4,1664]{1,0:T(4,128)(2,1)S(1)} %pack.1), channel_id=1, source_target_pairs={{0,16},{4,20},{8,24},{12,28},{16,0},{20,4},{24,8},{28,12},{1,17},{... | collective-permute-start | bytes 39944 | tf_op jit(solution)/shard_map/ppermute | solution.py:27
  6.6 3.9 %collective-permute-start.1 = (bf16[8,1664]{1,0:T(8,128)(2,1)S(1)}, bf16[8,1664]{1,0:T(8,128)(2,1)S(1)}, u32[]{:S(2)}, u32[]{:S(2)}) collective-permute-start(bf16[8,1664]{1,0:T(8,128)(2,1)S(1)} %pad_maximum_fusion.2), channel_id=1, source_target_pairs={{0,8},{4,12},{8,0},{12,4},{16,24},{20,28},{24,16},{28,20},{1,9},{5... | collective-permute-start | bytes 79880 | tf_op jit(solution)/shard_map/ppermute | solution.py:27
  10.5 7.8 %collective-permute-start.2 = (bf16[16,1664]{1,0:T(8,128)(2,1)S(1)}, bf16[16,1664]{1,0:T(8,128)(2,1)S(1)}, u32[]{:S(2)}, u32[]{:S(2)}) collective-permute-start(bf16[16,1664]{1,0:T(8,128)(2,1)S(1)} %pad_maximum_fusion.1), channel_id=1, source_target_pairs={{0,4},{4,0},{8,12},{12,8},{16,20},{20,16},{24,28},{28,24},{1,5},{5... | collective-permute-start | bytes 159752 | tf_op jit(solution)/shard_map/ppermute | solution.py:27
  16.3 2.0 %copy-start = (bf16[1536,8]{0,1:T(8,128)(2,1)S(1)}, bf16[1536,8]{0,1:T(8,128)(2,1)}, u32[]{:S(2)}) copy-start(bf16[1536,8]{0,1:T(8,128)(2,1)} %param.8) | copy-start | bytes 73732
  27.9 9.3 %collective-permute-start.3 = (f32[2,2,32,1152]{3,2,1,0:T(8,128)S(1)}, f32[2,2,32,1152]{3,2,1,0:T(8,128)S(1)}, u32[]{:S(2)}, u32[]{:S(2)}) collective-permute-start(f32[2,2,32,1152]{3,2,1,0:T(8,128)S(1)} %get-tuple-element.14), channel_id=1, source_target_pairs={{0,1},{1,0},{2,3},{3,2},{4,5},{5,4},{6,7},{7,6},{8,9},{9,8},{10,11... | collective-permute-start | bytes 1769480 | tf_op jit(solution)/shard_map/ppermute | solution.py:27
  37.3 8.8 %collective-permute-start.5 = (bf16[2,2,32,1024]{3,2,1,0:T(8,128)(2,1)S(1)}, bf16[2,2,32,1024]{3,2,1,0:T(8,128)(2,1)S(1)}, u32[]{:S(2)}, u32[]{:S(2)}) collective-permute-start(bf16[2,2,32,1024]{3,2,1,0:T(8,128)(2,1)S(1)} %get-tuple-element.23), channel_id=1, source_target_pairs={{0,2},{1,3},{2,0},{3,1},{4,6},{5,7},{6,4},{7,5},{8,10},{9,11},{10,... | collective-permute-start | bytes 786440 | tf_op jit(solution)/shard_map/ppermute | solution.py:27
  46.1 11.9 %collective-permute-start.6 = (bf16[2,32,1024]{2,1,0:T(8,128)(2,1)S(1)}, bf16[2,32,1024]{2,1,0:T(8,128)(2,1)S(1)}, u32[]{:S(2)}, u32[]{:S(2)}) collective-permute-start(bf16[2,32,1024]{2,1,0:T(8,128)(2,1)S(1)} %silu_times_up.1.hidden_ref), channel_id=1, source_target_pairs={{0,1},{1,0},{2,3},{3,2},{4,5},{5,4},{6,7},{7,6},{8,9},{9,8},{10,11... | collective-permute-start | bytes 393224 | tf_op jit(solution)/shard_map/ppermute | solution.py:27
  46.2 8.2 %collective-permute-start.4 = (f32[32,8]{1,0:T(8,128)S(1)}, f32[32,8]{1,0:T(8,128)S(1)}, u32[]{:S(2)}, u32[]{:S(2)}) collective-permute-start(f32[32,8]{1,0:T(8,128)S(1)} %fusion.1.near_ref), channel_id=1, source_target_pairs={{0,2},{1,3},{2,0},{3,1},{4,6},{5,7},{6,4},{7,5},{8,10},{9,11},{10,... | collective-permute-start | bytes 3080 | tf_op jit(solution)/shard_map/ppermute | solution.py:27
  61.8 4.2 %collective-permute-start.7 = (bf16[16,1536]{1,0:T(8,128)(2,1)S(1)}, bf16[16,1536]{1,0:T(8,128)(2,1)S(1)}, u32[]{:S(2)}, u32[]{:S(2)}) collective-permute-start(bf16[16,1536]{1,0:T(8,128)(2,1)S(1)} %get-tuple-element.22), channel_id=1, source_target_pairs={{0,4},{4,0},{8,12},{12,8},{16,20},{20,16},{24,28},{28,24},{1,5},{5... | collective-permute-start | bytes 147464 | tf_op jit(solution)/shard_map/ppermute | solution.py:27
  66.0 3.9 %collective-permute-start.8 = (bf16[8,1536]{1,0:T(8,128)(2,1)S(1)}, bf16[8,1536]{1,0:T(8,128)(2,1)S(1)}, u32[]{:S(2)}, u32[]{:S(2)}) collective-permute-start(bf16[8,1536]{1,0:T(8,128)(2,1)S(1)} %slice.47), channel_id=1, source_target_pairs={{0,8},{4,12},{8,0},{12,4},{16,24},{20,28},{24,16},{28,20},{1,9},{5... | collective-permute-start | bytes 73736 | tf_op jit(solution)/shard_map/ppermute | solution.py:27
  69.9 4.7 %collective-permute-start.9 = (bf16[4,1536]{1,0:T(4,128)(2,1)S(1)}, bf16[4,1536]{1,0:T(4,128)(2,1)S(1)}, u32[]{:S(2)}, u32[]{:S(2)}) collective-permute-start(bf16[4,1536]{1,0:T(4,128)(2,1)S(1)} %slice.48), channel_id=1, source_target_pairs={{0,16},{4,20},{8,24},{12,28},{16,0},{20,4},{24,8},{28,12},{1,17},{... | collective-permute-start | bytes 36872 | tf_op jit(solution)/shard_map/ppermute | solution.py:27

commit v4 on v3

--- a/solution.py
+++ b/solution.py
@@ -10,7 +10,7 @@
 
 LANES = 128
 MIB = 1 << 20
-WINDOWS = 3
+BESIDE = (1, 2, 2)
 AHEAD = 2
 SLOTS = 8
 VMEM = pl.BlockSpec(memory_space=pltpu.VMEM)
@@ -94,24 +94,26 @@
             block_copy(gate_hbm, up_hbm, number, kind, ring, sems).start()
 
 
-def load_first_kernel(number, gate_hbm, up_hbm, *refs):
+def load_first_kernel(begin, stop, gate_hbm, up_hbm, *refs):
     ring, sems = refs[-2:]
-    start_block(gate_hbm, up_hbm, number, ring, sems)
-    block_copy(gate_hbm, up_hbm, number, 0, ring, sems).wait()
-
-
-def load_first(number, w_gate, w_up, ring):
+    for number in range(begin, stop):
+        start_block(gate_hbm, up_hbm, number, ring, sems)
+    for number in range(begin, stop):
+        block_copy(gate_hbm, up_hbm, number, 0, ring, sems).wait()
+
+
+def load_first(begin, stop, w_gate, w_up, ring):
     width, half = w_gate.shape[1], w_gate.shape[2] // 2
     slots = min(SLOTS, 2 * w_gate.shape[0])
     return pl.pallas_call(
-        functools.partial(load_first_kernel, number),
+        functools.partial(load_first_kernel, begin, stop),
         out_shape=pltpu.VMEM((slots, width, half), w_gate.dtype),
         in_specs=[HBM, HBM] + ([] if ring is None else [VMEM]),
         out_specs=VMEM,
         input_output_aliases={} if ring is None else {2: 0},
         scratch_shapes=[pltpu.SemaphoreType.DMA((slots,))],
         compiler_params=pltpu.CompilerParams(vmem_limit_bytes=MIB),
-        cost_estimate=cost(0, 2 * width * half),
+        cost_estimate=cost(0, 2 * (stop - begin) * width * half),
     )(w_gate, w_up, *([] if ring is None else [ring]))
 
 
@@ -305,10 +307,10 @@
     w_gate, w_up, w_down = (
         pltpu.with_memory_space_constraint(w, pltpu.HBM) for w in (w_gate, w_up, w_down)
     )
-    early = min(WINDOWS, len(bits))
-    ring = None
-    for i in range(early):
-        ring = load_first(i, w_gate, w_up, ring)
+    early, ring = 0, None
+    for blocks in BESIDE[: len(bits)]:
+        ring = load_first(early, early + blocks, w_gate, w_up, ring)
+        early += blocks
     x = pack(tokens, expert_ids)
     for bit in reversed(bits):
         x = jnp.concatenate([x, swap(x, "dp", bit)], axis=0)

time: 75.4 us -> 75.5 us (level)
    pallas_call x3, Pallas kernels: 5.91 us -> 7.82 us  [load_first(): pl.pallas_call(functools.partial(load_first_kernel, begin, stop), out_sha...]
    pallas_call x2, Pallas kernels: 18.7 us -> 16.9 us  [gate_up(): pl.pallas_call(functools.partial(gate_up_kernel, 2 * experts if mine else...]
  transfers between devices with their start and end apart: 10 -> 10, of which waited for: 6 -> 6; matrix products, arithmetic and copies ran while one was open for 0% -> 0% of each run, Pallas kernels for 34% -> 36%
where the time goes in v4:
time: 75.5 us; the launch traced here: 75.3 us
  Pallas kernels  39.6 us (52%)
  waiting for transfers between devices  18.7 us (25%)
  starting transfers between devices  16.1 us (21%)
    ppermute x10, waiting for transfers between devices, swap(): return lax.ppermute(value, axis, [(i, i ^ bit) for i in range(count)])  18.7 us
    pallas_call x2, Pallas kernels, gate_up(): pl.pallas_call(functools.partial(gate_up_kernel, 2 * experts if mine else...  16.9 us
    ppermute x10, starting transfers between devices, swap(): return lax.ppermute(value, axis, [(i, i ^ bit) for i in range(count)])  16.1 us
    pallas_call x3, Pallas kernels, load_first(): pl.pallas_call(functools.partial(load_first_kernel, begin, stop), out_sha...  7.82 us
    pallas_call x2, Pallas kernels, down(): pl.pallas_call(functools.partial(down_kernel, last, begin, count), out_sh...  7.39 us
    pallas_call x1, Pallas kernels, load_down(): pl.pallas_call(functools.partial(load_down_kernel, count), out_shape=(sid...  6.57 us
  transfers between devices with their start and end apart: 10, of which 6 were waited for; matrix products, arithmetic and copies ran while one was open for 0% of the time, Pallas kernels for 36%

profile of v4, /device:TPU:0, one launch (start us, length us, event | category | flops | bytes accessed | tf_op | source)
XLA Modules:
  0.0 75.3 jit_solution(11821393000475582417)
XLA Ops:
  0.0 0.8 %pack.1 = bf16[4,1664]{1,0:T(4,128)(2,1)S(1)} custom-call(bf16[4,1536]{1,0:T(4,128)(2,1)} %token_hbm.1, s32[2,4]{1,0:T(2,128)} %bitcast.5), custom_call_target="tpu_custom_call" | custom-call | tf_op jit(solution)/shard_map/pack/pallas_call | solution.py:55
  0.8 4.1 %collective-permute-start = (bf16[4,1664]{1,0:T(4,128)(2,1)S(1)}, bf16[4,1664]{1,0:T(4,128)(2,1)S(1)}, u32[]{:S(2)}, u32[]{:S(2)}) collective-permute-start(bf16[4,1664]{1,0:T(4,128)(2,1)S(1)} %pack.1), channel_id=1, source_target_pairs={{0,16},{4,20},{8,24},{12,28},{16,0},{20,4},{24,8},{28,12},{1,17},{... | collective-permute-start | bytes 39944 | tf_op jit(solution)/shard_map/ppermute | solution.py:27
  4.9 1.7 %collective-permute-done = bf16[4,1664]{1,0:T(4,128)(2,1)S(1)} collective-permute-done((bf16[4,1664]{1,0:T(4,128)(2,1)S(1)}, bf16[4,1664]{1,0:T(4,128)(2,1)S(1)}, u32[]{:S(2)}, u32[]{:S(2)}) %collective-permute-start) | collective-permute-done | bytes 13344 | tf_op jit(solution)/shard_map/ppermute | solution.py:27
  6.6 2.0 %collective-permute-start.1 = (bf16[8,1664]{1,0:T(8,128)(2,1)S(1)}, bf16[8,1664]{1,0:T(8,128)(2,1)S(1)}, u32[]{:S(2)}, u32[]{:S(2)}) collective-permute-start(bf16[8,1664]{1,0:T(8,128)(2,1)S(1)} %pad_maximum_fusion.2), channel_id=1, source_target_pairs={{0,8},{4,12},{8,0},{12,4},{16,24},{20,28},{24,16},{28,20},{1,9},{5... | collective-permute-start | bytes 79880 | tf_op jit(solution)/shard_map/ppermute | solution.py:27
  8.6 1.9 %collective-permute-done.1 = bf16[8,1664]{1,0:T(8,128)(2,1)S(1)} collective-permute-done((bf16[8,1664]{1,0:T(8,128)(2,1)S(1)}, bf16[8,1664]{1,0:T(8,128)(2,1)S(1)}, u32[]{:S(2)}, u32[]{:S(2)}) %collective-permute-start.1) | collective-permute-done | bytes 26656 | tf_op jit(solution)/shard_map/ppermute | solution.py:27
  10.5 1.8 %collective-permute-start.2 = (bf16[16,1664]{1,0:T(8,128)(2,1)S(1)}, bf16[16,1664]{1,0:T(8,128)(2,1)S(1)}, u32[]{:S(2)}, u32[]{:S(2)}) collective-permute-start(bf16[16,1664]{1,0:T(8,128)(2,1)S(1)} %pad_maximum_fusion.1), channel_id=1, source_target_pairs={{0,4},{4,0},{8,12},{12,8},{16,20},{20,16},{24,28},{28,24},{1,5},{5... | collective-permute-start | bytes 159752 | tf_op jit(solution)/shard_map/ppermute | solution.py:27
  12.4 2.0 %shard_map.64.refs_0_ = bf16[8,1536,1024]{2,1,0:T(8,128)(2,1)S(1)} custom-call(bf16[5,1536,2048]{2,1,0:T(8,128)(2,1)} %gate_hbm.9, bf16[5,1536,2048]{2,1,0:T(8,128)(2,1)} %up_hbm.9), custom_call_target="tpu_custom_call" | custom-call | bytes 3145728 | tf_op jit(solution)/shard_map/pallas_call | solution.py:108
  14.4 2.9 %shard_map.65.refs_0_ = bf16[8,1536,1024]{2,1,0:T(8,128)(2,1)S(1)} custom-call(bf16[5,1536,2048]{2,1,0:T(8,128)(2,1)} %gate_hbm.9, bf16[5,1536,2048]{2,1,0:T(8,128)(2,1)} %up_hbm.9, bf16[8,1536,1024]{2,1,0:T(8,128)(2,1)S(1)} %shard_map.64.refs_0_), custom_call_target="tpu_custom_call", output_to_operand_aliasing={{}: (2, {})} | custom-call | bytes 6291456 | tf_op jit(solution)/shard_map/pallas_call | solution.py:108
  17.3 0.0 copy-start
  17.3 2.9 %shard_map.66._ = bf16[8,1536,1024]{2,1,0:T(8,128)(2,1)S(1)} custom-call(bf16[5,1536,2048]{2,1,0:T(8,128)(2,1)} %gate_hbm.9, bf16[5,1536,2048]{2,1,0:T(8,128)(2,1)} %up_hbm.9, bf16[8,1536,1024]{2,1,0:T(8,128)(2,1)S(1)} %shard_map.65.refs_0_), custom_call_target="tpu_custom_call", output_to_operand_aliasing={{}: (2, {})} | custom-call | bytes 6291456 | tf_op jit(solution)/shard_map/pallas_call | solution.py:108
  20.2 0.0 collective-permute-done.2
  20.3 7.7 %gate_up_other.1 = (f32[2,2,32,1152]{3,2,1,0:T(8,128)S(1)}, bf16[8,1536,1024]{2,1,0:T(8,128)(2,1)S(1)}) custom-call(bf16[32,1664]{1,0:T(8,128)(2,1)S(1)} %pad_maximum_fusion.x_ref, bf16[5,1536,2048]{2,1,0:T(8,128)(2,1)} %gate_hbm.9, bf16[5,1536,2048]{2,1,0:T(8,128)(2,1)} %up_hbm.9, ...), custom_call_target="tpu_custom_call", output_to_operand_aliasing={{1}: (3, {})} | custom-call | flops 1006632960 | bytes 22020096 | tf_op jit(solution)/shard_map/gate_up_other/pallas_call | solution.py:166
  28.0 0.1 collective-permute-start.3
  28.1 9.2 %gate_up_mine.1 = (f32[2,2,32,1024]{3,2,1,0:T(8,128)S(1)}, bf16[8,1536,1024]{2,1,0:T(8,128)(2,1)S(1)}) custom-call(bf16[32,1664]{1,0:T(8,128)(2,1)S(1)} %pad_maximum_fusion.x_ref, bf16[5,1536,2048]{2,1,0:T(8,128)(2,1)} %gate_hbm.9, bf16[5,1536,2048]{2,1,0:T(8,128)(2,1)} %up_hbm.9, ...), custom_call_target="tpu_custom_call", output_to_operand_aliasing={{1}: (3, {})} | custom-call | flops 1006632960 | bytes 25165824 | tf_op jit(solution)/shard_map/gate_up_mine/pallas_call | solution.py:166
  37.3 0.0 collective-permute-done.3
  37.3 0.1 fusion.2
  37.4 1.6 %collective-permute-start.5 = (bf16[2,2,32,1024]{3,2,1,0:T(8,128)(2,1)S(1)}, bf16[2,2,32,1024]{3,2,1,0:T(8,128)(2,1)S(1)}, u32[]{:S(2)}, u32[]{:S(2)}) collective-permute-start(bf16[2,2,32,1024]{3,2,1,0:T(8,128)(2,1)S(1)} %get-tuple-element.23), channel_id=1, source_target_pairs={{0,2},{1,3},{2,0},{3,1},{4,6},{5,7},{6,4},{7,5},{8,10},{9,11},{10,... | collective-permute-start | bytes 786440 | tf_op jit(solution)/shard_map/ppermute | solution.py:27
  39.0 7.2 %collective-permute-done.5.far_ref = bf16[2,2,32,1024]{3,2,1,0:T(8,128)(2,1)S(1)} collective-permute-done((bf16[2,2,32,1024]{3,2,1,0:T(8,128)(2,1)S(1)}, bf16[2,2,32,1024]{3,2,1,0:T(8,128)(2,1)S(1)}, u32[]{:S(2)}, u32[]{:S(2)}) %collective-permute-start.5) | collective-permute-done | bytes 262176 | tf_op jit(solution)/shard_map/ppermute | solution.py:27
  46.1 0.1 silu_times_up.1.hidden_ref
  46.2 0.1 collective-permute-start.6
  46.3 1.6 %collective-permute-start.4 = (f32[32,8]{1,0:T(8,128)S(1)}, f32[32,8]{1,0:T(8,128)S(1)}, u32[]{:S(2)}, u32[]{:S(2)}) collective-permute-start(f32[32,8]{1,0:T(8,128)S(1)} %fusion.1.near_ref), channel_id=1, source_target_pairs={{0,2},{1,3},{2,0},{3,1},{4,6},{5,7},{6,4},{7,5},{8,10},{9,11},{10,... | collective-permute-start | bytes 3080 | tf_op jit(solution)/shard_map/ppermute | solution.py:27
  47.9 6.6 %load_down.1 = (bf16[5,1024,1536]{2,1,0:T(8,128)(2,1)S(1)}, bf16[5,1024,1536]{2,1,0:T(8,128)(2,1)S(1)}) custom-call(bf16[5,2048,1536]{2,1,0:T(8,128)(2,1)} %down_hbm.5), custom_call_target="tpu_custom_call" | custom-call | bytes 18874368 | tf_op jit(solution)/shard_map/load_down/pallas_call | solution.py:225
  54.5 0.0 collective-permute-done.4.far_ref
  54.5 3.7 %down_mine.1 = (f32[32,1536]{1,0:T(8,128)S(1)}, bf16[5,1024,1536]{2,1,0:T(8,128)(2,1)S(1)}) custom-call(bf16[32,1664]{1,0:T(8,128)(2,1)S(1)} %pad_maximum_fusion.x_ref, f32[32,8]{1,0:T(8,128)S(1)} %fusion.1.near_ref, f32[32,8]{1,0:T(8,128)S(1)} %collective-permute-done.4.far_ref, ...), custom_call_target="tpu_custom_call", output_to_operand_aliasing={{1}: (6, {})} | custom-call | flops 503316480 | bytes 6291456 | tf_op jit(solution)/shard_map/down_mine/pallas_call | solution.py:290
  58.2 3.7 %down_last.1 = (f32[16,1536]{1,0:T(8,128)S(1)}, bf16[16,1536]{1,0:T(8,128)(2,1)S(1)}, bf16[5,1024,1536]{2,1,0:T(8,128)(2,1)S(1)}) custom-call(bf16[32,1664]{1,0:T(8,128)(2,1)S(1)} %pad_maximum_fusion.x_ref, f32[32,8]{1,0:T(8,128)S(1)} %fusion.1.near_ref, f32[32,8]{1,0:T(8,128)S(1)} %collective-permute-done.4.far_ref, ...), custom_call_target="tpu_custom_call", output_to_operand_aliasing={{2}: (5, {})} | custom-call | flops 503316480 | bytes 6291456 | tf_op jit(solution)/shard_map/down_last/pallas_call | solution.py:290
  61.9 0.6 collective-permute-start.7
  62.5 3.6 %collective-permute-done.7 = bf16[16,1536]{1,0:T(8,128)(2,1)S(1)} collective-permute-done((bf16[16,1536]{1,0:T(8,128)(2,1)S(1)}, bf16[16,1536]{1,0:T(8,128)(2,1)S(1)}, u32[]{:S(2)}, u32[]{:S(2)}) %collective-permute-start.7) | collective-permute-done | bytes 49184 | tf_op jit(solution)/shard_map/ppermute | solution.py:27
  66.1 1.6 %collective-permute-start.8 = (bf16[8,1536]{1,0:T(8,128)(2,1)S(1)}, bf16[8,1536]{1,0:T(8,128)(2,1)S(1)}, u32[]{:S(2)}, u32[]{:S(2)}) collective-permute-start(bf16[8,1536]{1,0:T(8,128)(2,1)S(1)} %slice.47), channel_id=1, source_target_pairs={{0,8},{4,12},{8,0},{12,4},{16,24},{20,28},{24,16},{28,20},{1,9},{5... | collective-permute-start | bytes 73736 | tf_op jit(solution)/shard_map/ppermute | solution.py:27
  67.7 2.3 %collective-permute-done.8 = bf16[8,1536]{1,0:T(8,128)(2,1)S(1)} collective-permute-done((bf16[8,1536]{1,0:T(8,128)(2,1)S(1)}, bf16[8,1536]{1,0:T(8,128)(2,1)S(1)}, u32[]{:S(2)}, u32[]{:S(2)}) %collective-permute-start.8) | collective-permute-done | bytes 24608 | tf_op jit(solution)/shard_map/ppermute | solution.py:27
  70.0 2.6 %collective-permute-start.9 = (bf16[4,1536]{1,0:T(4,128)(2,1)S(1)}, bf16[4,1536]{1,0:T(4,128)(2,1)S(1)}, u32[]{:S(2)}, u32[]{:S(2)}) collective-permute-start(bf16[4,1536]{1,0:T(4,128)(2,1)S(1)} %slice.48), channel_id=1, source_target_pairs={{0,16},{4,20},{8,24},{12,28},{16,0},{20,4},{24,8},{28,12},{1,17},{... | collective-permute-start | bytes 36872 | tf_op jit(solution)/shard_map/ppermute | solution.py:27
  72.7 2.0 %collective-permute-done.9 = bf16[4,1536]{1,0:T(4,128)(2,1)S(1)} collective-permute-done((bf16[4,1536]{1,0:T(4,128)(2,1)S(1)}, bf16[4,1536]{1,0:T(4,128)(2,1)S(1)}, u32[]{:S(2)}, u32[]{:S(2)}) %collective-permute-start.9) | collective-permute-done | bytes 12320 | tf_op jit(solution)/shard_map/ppermute | solution.py:27
  74.7 0.6 fusion
  (10 shorter events, 0.1 us)
Async XLA Ops:
  0.8 5.8 %collective-permute-start = (bf16[4,1664]{1,0:T(4,128)(2,1)S(1)}, bf16[4,1664]{1,0:T(4,128)(2,1)S(1)}, u32[]{:S(2)}, u32[]{:S(2)}) collective-permute-start(bf16[4,1664]{1,0:T(4,128)(2,1)S(1)} %pack.1), channel_id=1, source_target_pairs={{0,16},{4,20},{8,24},{12,28},{16,0},{20,4},{24,8},{28,12},{1,17},{... | collective-permute-start | bytes 39944 | tf_op jit(solution)/shard_map/ppermute | solution.py:27
  6.6 3.9 %collective-permute-start.1 = (bf16[8,1664]{1,0:T(8,128)(2,1)S(1)}, bf16[8,1664]{1,0:T(8,128)(2,1)S(1)}, u32[]{:S(2)}, u32[]{:S(2)}) collective-permute-start(bf16[8,1664]{1,0:T(8,128)(2,1)S(1)} %pad_maximum_fusion.2), channel_id=1, source_target_pairs={{0,8},{4,12},{8,0},{12,4},{16,24},{20,28},{24,16},{28,20},{1,9},{5... | collective-permute-start | bytes 79880 | tf_op jit(solution)/shard_map/ppermute | solution.py:27
  10.5 9.7 %collective-permute-start.2 = (bf16[16,1664]{1,0:T(8,128)(2,1)S(1)}, bf16[16,1664]{1,0:T(8,128)(2,1)S(1)}, u32[]{:S(2)}, u32[]{:S(2)}) collective-permute-start(bf16[16,1664]{1,0:T(8,128)(2,1)S(1)} %pad_maximum_fusion.1), channel_id=1, source_target_pairs={{0,4},{4,0},{8,12},{12,8},{16,20},{20,16},{24,28},{28,24},{1,5},{5... | collective-permute-start | bytes 159752 | tf_op jit(solution)/shard_map/ppermute | solution.py:27
  17.3 3.0 %copy-start = (bf16[1536,8]{0,1:T(8,128)(2,1)S(1)}, bf16[1536,8]{0,1:T(8,128)(2,1)}, u32[]{:S(2)}) copy-start(bf16[1536,8]{0,1:T(8,128)(2,1)} %param.8) | copy-start | bytes 73732
  28.0 9.3 %collective-permute-start.3 = (f32[2,2,32,1152]{3,2,1,0:T(8,128)S(1)}, f32[2,2,32,1152]{3,2,1,0:T(8,128)S(1)}, u32[]{:S(2)}, u32[]{:S(2)}) collective-permute-start(f32[2,2,32,1152]{3,2,1,0:T(8,128)S(1)} %get-tuple-element.14), channel_id=1, source_target_pairs={{0,1},{1,0},{2,3},{3,2},{4,5},{5,4},{6,7},{7,6},{8,9},{9,8},{10,11... | collective-permute-start | bytes 1769480 | tf_op jit(solution)/shard_map/ppermute | solution.py:27
  37.4 8.8 %collective-permute-start.5 = (bf16[2,2,32,1024]{3,2,1,0:T(8,128)(2,1)S(1)}, bf16[2,2,32,1024]{3,2,1,0:T(8,128)(2,1)S(1)}, u32[]{:S(2)}, u32[]{:S(2)}) collective-permute-start(bf16[2,2,32,1024]{3,2,1,0:T(8,128)(2,1)S(1)} %get-tuple-element.23), channel_id=1, source_target_pairs={{0,2},{1,3},{2,0},{3,1},{4,6},{5,7},{6,4},{7,5},{8,10},{9,11},{10,... | collective-permute-start | bytes 786440 | tf_op jit(solution)/shard_map/ppermute | solution.py:27
  46.2 11.9 %collective-permute-start.6 = (bf16[2,32,1024]{2,1,0:T(8,128)(2,1)S(1)}, bf16[2,32,1024]{2,1,0:T(8,128)(2,1)S(1)}, u32[]{:S(2)}, u32[]{:S(2)}) collective-permute-start(bf16[2,32,1024]{2,1,0:T(8,128)(2,1)S(1)} %silu_times_up.1.hidden_ref), channel_id=1, source_target_pairs={{0,1},{1,0},{2,3},{3,2},{4,5},{5,4},{6,7},{7,6},{8,9},{9,8},{10,11... | collective-permute-start | bytes 393224 | tf_op jit(solution)/shard_map/ppermute | solution.py:27
  46.3 8.2 %collective-permute-start.4 = (f32[32,8]{1,0:T(8,128)S(1)}, f32[32,8]{1,0:T(8,128)S(1)}, u32[]{:S(2)}, u32[]{:S(2)}) collective-permute-start(f32[32,8]{1,0:T(8,128)S(1)} %fusion.1.near_ref), channel_id=1, source_target_pairs={{0,2},{1,3},{2,0},{3,1},{4,6},{5,7},{6,4},{7,5},{8,10},{9,11},{10,... | collective-permute-start | bytes 3080 | tf_op jit(solution)/shard_map/ppermute | solution.py:27
  61.9 4.2 %collective-permute-start.7 = (bf16[16,1536]{1,0:T(8,128)(2,1)S(1)}, bf16[16,1536]{1,0:T(8,128)(2,1)S(1)}, u32[]{:S(2)}, u32[]{:S(2)}) collective-permute-start(bf16[16,1536]{1,0:T(8,128)(2,1)S(1)} %get-tuple-element.22), channel_id=1, source_target_pairs={{0,4},{4,0},{8,12},{12,8},{16,20},{20,16},{24,28},{28,24},{1,5},{5... | collective-permute-start | bytes 147464 | tf_op jit(solution)/shard_map/ppermute | solution.py:27
  66.1 3.9 %collective-permute-start.8 = (bf16[8,1536]{1,0:T(8,128)(2,1)S(1)}, bf16[8,1536]{1,0:T(8,128)(2,1)S(1)}, u32[]{:S(2)}, u32[]{:S(2)}) collective-permute-start(bf16[8,1536]{1,0:T(8,128)(2,1)S(1)} %slice.47), channel_id=1, source_target_pairs={{0,8},{4,12},{8,0},{12,4},{16,24},{20,28},{24,16},{28,20},{1,9},{5... | collective-permute-start | bytes 73736 | tf_op jit(solution)/shard_map/ppermute | solution.py:27
  70.0 4.7 %collective-permute-start.9 = (bf16[4,1536]{1,0:T(4,128)(2,1)S(1)}, bf16[4,1536]{1,0:T(4,128)(2,1)S(1)}, u32[]{:S(2)}, u32[]{:S(2)}) collective-permute-start(bf16[4,1536]{1,0:T(4,128)(2,1)S(1)} %slice.48), channel_id=1, source_target_pairs={{0,16},{4,20},{8,24},{12,28},{16,0},{20,4},{24,8},{28,12},{1,17},{... | collective-permute-start | bytes 36872 | tf_op jit(solution)/shard_map/ppermute | solution.py:27
